TPU v7x, 256 devices: a whole 4x4x8 slice. The times are simulated.
256 devices in a mesh: space: 64 (over z, x, core), rep: 4 (over y).
Axes of the slice: x: 4, y: 4, z: 8, core: 2. Of those that a mesh axis runs over, the one named last changes fastest.
Arguments:
- features: bfloat16 [4, 32768, 256], P('rep', 'space'), may hold values from -6 to 6
- neighbours: int32 [4, 32768, 27], P('rep', 'space'), may hold values from -1 to 32767, as said below
- serial: int32 [4, 32768], P('rep', 'space'), may hold values from 0 to 32767, as said below
- w_conv: bfloat16 [6912, 256], replicated, may hold values from -0.078125 to 0.078125
- w_qkv: bfloat16 [256, 768], replicated, may hold values from -45 to 45
- w_proj: bfloat16 [256, 256], replicated, may hold values from -0.375 to 0.375
- cotangent: bfloat16 [4, 32768, 256], P('rep', 'space'), may hold values from -6 to 6
Outputs:
- output: bfloat16 [4, 32768, 256], P('rep', 'space')
- g_conv: float32 [6912, 256], P('space')
- g_qkv: float32 [256, 768], P('space')
- g_proj: float32 [256, 256], P('space')
Inputs may be any that keep to these rules, and one draw needn't show every extreme that they name: `neighbours`: entry k of a voxel's row names the row (within its window, slab after slab of 512 rows) of its neighbour at the k-th of 27 offsets, or -1 where there is none; entry 13 is the voxel itself. A neighbour lies in the voxel's own slab, in the last 128 rows of the slab below, or in the first 128 rows of the slab above. `serial`: each window's row is a permutation. The voxels of one slab take at most 16 of the positions of one aligned block of 512 serialized positions, and every slab takes exactly 16 in some block.
All inputs are finite; a program needn't handle non-finite values.
Results may differ from a plain program's by a relative error of at most 0.02.
The roundings to bfloat16 on the way count: a program that leaves them out, or rounds other values in their place, can miss the bound.
Values may be sent and summed in bfloat16 or wider, within the bound.
No kernel may reach another device: no remote copies, remote signals or barrier semaphores. Data moves between devices by JAX's collectives and lax.ppermute only.
A program may use at most 64 MiB of HBM per device.

v0:
```python
import functools

import jax
import jax.numpy as jnp
from jax import lax
from jax.experimental import pallas as pl
from jax.experimental.pallas import tpu as pltpu
from jax.sharding import Mesh
from jax.sharding import PartitionSpec as P


HEADS = 8
RIM = 128
EPSILON = 1e-05
SPACE = ("z", "x", "c")
VACANT = 512.0
OFFSETS_PER_STEP = 3

F32 = jnp.float32
BF16 = jnp.bfloat16


def iota(shape, dim):
    return lax.broadcasted_iota(jnp.int32, shape, dim)


def mm(a, b):
    return jnp.dot(a, b, preferred_element_type=F32)


def mm_nt(a, b):
    return lax.dot_general(a, b, (((1,), (1,)), ((), ())), preferred_element_type=F32)


def mm_tn(a, b):
    return lax.dot_general(a, b, (((0,), (0,)), ((), ())), preferred_element_type=F32)


def one_hot(mask):
    return jnp.where(mask, 1.0, 0.0).astype(BF16)


def turned(a):
    return jnp.transpose(a.astype(F32), (1, 0))


def cost(flops, nbytes):
    return pl.CostEstimate(flops=int(flops), bytes_accessed=int(nbytes), transcendentals=0)


VMEM_SPEC = pl.BlockSpec(memory_space=pltpu.VMEM)


def in_hbm(a):
    return pltpu.with_memory_space_constraint(a, pltpu.HBM)


def params(mebibytes, **more):
    return pltpu.CompilerParams(vmem_limit_bytes=mebibytes << 20, **more)


def slots_of(serial, capacity, owners):
    length = serial.shape[1]
    owner = lax.div(serial, jnp.int32(length))
    member = iota((owners, length), 0) == owner
    before = one_hot(iota((length, length), 0) < iota((length, length), 1))
    earlier = mm(one_hot(member), before)
    place = earlier + (capacity * iota((owners, length), 0)).astype(F32)
    return jnp.sum(jnp.where(member, place, 0.0), axis=0, keepdims=True)


def conv_kernel(
    capacity,
    serial_ref,
    cot_ref,
    nb_ref,
    below_ref,
    own_ref,
    above_ref,
    w_ref,
    g_ref,
    buf_ref,
    slot_ref,
    table,
    acc,
):
    step = pl.program_id(0)
    length, channels = own_ref.shape
    slots = buf_ref.shape[0]
    rows = table.shape[1]
    index = (lax.axis_index("z") * lax.axis_size("x") + lax.axis_index("x")) * lax.axis_size(
        "c"
    ) + lax.axis_index("c")
    base = index * length - RIM

    @pl.when(step == 0)
    def _():
        table[:, :RIM] = turned(below_ref[...]).astype(BF16)
        table[:, RIM : RIM + length] = turned(own_ref[...]).astype(BF16)
        table[:, RIM + length :] = turned(above_ref[...]).astype(BF16)
        acc[...] = jnp.zeros_like(acc)

    total = acc[...]
    for j in range(nb_ref.shape[0]):
        linked = nb_ref[j]
        local = jnp.where(linked < 0, -1, linked - base)
        pick = one_hot(iota((rows, length), 0) == local)
        gathered = mm(table[...], pick).astype(BF16)
        g_ref[j * channels : (j + 1) * channels, :] = gathered
        total = total + mm_tn(w_ref[j * channels : (j + 1) * channels, :], gathered)
    acc[...] = total

    @pl.when(step == pl.num_programs(0) - 1)
    def _():
        mixed = (own_ref[...].astype(F32) + turned(acc[...])).astype(BF16)
        slot = slots_of(serial_ref[...], capacity, slots // capacity)
        slot_ref[...] = jnp.broadcast_to(slot, slot_ref.shape)
        mask = iota((slots, length), 0) == slot.astype(jnp.int32)
        taken = jnp.sum(jnp.where(mask, 1.0, 0.0), axis=1, keepdims=True)
        vacant = jnp.where(taken > 0.5, 0.0, VACANT)
        pick = one_hot(mask)
        buf_ref[:, :channels] = mm(pick, mixed).astype(BF16)
        buf_ref[:, channels:] = (mm(pick, cot_ref[...]) + vacant).astype(BF16)


def gather_conv(serial, cot, nb, below, own, above, w_conv, slots, capacity):
    length, channels = own.shape
    count = nb.shape[0]
    per = OFFSETS_PER_STEP
    rows = length + 2 * RIM
    whole = lambda *shape: pl.BlockSpec(shape, lambda i: (0,) * len(shape))
    return pl.pallas_call(
        functools.partial(conv_kernel, capacity),
        grid=(count // per,),
        out_shape=(
            pltpu.HBM((count * channels, length), BF16),
            jax.ShapeDtypeStruct((slots, 2 * channels), BF16),
            jax.ShapeDtypeStruct((8, length), F32),
        ),
        in_specs=[
            whole(1, length),
            whole(length, channels),
            pl.BlockSpec((per, 1, length), lambda i: (i, 0, 0)),
            whole(RIM, channels),
            whole(length, channels),
            whole(RIM, channels),
            pl.BlockSpec((per * channels, channels), lambda i: (i, 0)),
        ],
        out_specs=(
            pl.BlockSpec((per * channels, length), lambda i: (i, 0)),
            whole(slots, 2 * channels),
            whole(8, length),
        ),
        scratch_shapes=[pltpu.VMEM((channels, rows), BF16), pltpu.VMEM((channels, length), F32)],
        compiler_params=params(32, dimension_semantics=("arbitrary",)),
        cost_estimate=cost(2 * count * length * channels * (rows + channels), 12 << 20),
        name="gather_conv",
    )(in_hbm(serial), in_hbm(cot), in_hbm(nb), below, in_hbm(own), above, in_hbm(w_conv))


def patch_kernel(
    buf_ref,
    wqkv_ref,
    wproj_ref,
    out_ref,
    dp_ref,
    gw_ref,
    key_s,
    value_s,
    query_s,
    datt_s,
    key_t,
    value_t,
    query_t,
    datt_t,
    att_t,
    dq_t,
    dk,
    dv,
):
    slots, channels = out_ref.shape
    groups, length, group = dk.shape
    depth = channels // HEADS
    factor = depth ** (-0.5)

    mark = buf_ref[:, channels : channels + 128][:, 0:1]
    valid = jnp.broadcast_to(mark.astype(F32), (slots, 128)) < VACANT / 2
    lower = one_hot(iota((slots, slots), 1) < iota((slots, slots), 0))
    col = jnp.where(valid, mm(lower, one_hot(valid)), -1.0)
    row = jnp.transpose(col, (1, 0))[0:1, :].astype(jnp.int32)
    rows = mm(one_hot(iota((length, slots), 0) == row), buf_ref[...])
    patched, upstream = rows[:, :channels], rows[:, channels:].astype(BF16)

    values_t = turned(patched)
    centre_t = values_t - jnp.mean(values_t, axis=0, keepdims=True)
    inverse = lax.rsqrt(jnp.mean(centre_t * centre_t, axis=0, keepdims=True) + EPSILON)
    centred_t = centre_t * inverse
    normed_t = centred_t.astype(BF16)
    w_qkv = wqkv_ref[...]
    qkv_t = mm_tn(w_qkv, normed_t)
    d_att = mm_nt(upstream, wproj_ref[...]).astype(BF16)
    query_t[...] = (qkv_t[:channels] * factor).astype(BF16)
    key_t[...] = qkv_t[channels : 2 * channels].astype(BF16)
    value_t[...] = qkv_t[2 * channels :].astype(BF16)
    datt_t[...] = turned(d_att).astype(BF16)
    for source, target in ((query_t, query_s), (key_t, key_s), (value_t, value_s)):
        flat = turned(source[...]).astype(BF16)
        for g in range(groups):
            target[g] = flat[:, g * group : (g + 1) * group]
    for g in range(groups):
        datt_s[g] = d_att[:, g * group : (g + 1) * group]

    lane = iota((length, group), 1)
    sub = iota((group, length), 0)
    zero = jnp.zeros((), BF16)

    def heads_of(g, carry):
        start = pl.multiple_of(g * group, group)
        k_g, v_g, q_g, da_g = key_s[g], value_s[g], query_s[g], datt_s[g]
        q_tg, da_tg = query_t[pl.ds(start, group), :], datt_t[pl.ds(start, group), :]
        dk_g = jnp.zeros((length, group), F32)
        dv_g = jnp.zeros((length, group), F32)
        for h in range(group // depth):
            in_rows = lax.div(sub, jnp.int32(depth)) == h
            in_lanes = lax.div(lane, jnp.int32(depth)) == h
            at = pl.ds(pl.multiple_of(start + h * depth, depth), depth)
            scores = mm(k_g, jnp.where(in_rows, q_tg, zero))
            e = jnp.exp(scores - jnp.max(scores, axis=0, keepdims=True))
            p = e * (1.0 / jnp.sum(e, axis=0, keepdims=True))
            pb = p.astype(BF16)
            att_t[at, :] = mm(value_t[at, :], pb)
            dv_g = dv_g + mm(pb, jnp.where(in_lanes, da_g, zero))
            dp = mm(v_g, jnp.where(in_rows, da_tg, zero))
            ds = (p * (dp - jnp.sum(dp * p, axis=0, keepdims=True))).astype(BF16)
            dq_t[at, :] = mm(key_t[at, :], ds)
            dk_g = dk_g + mm(ds, jnp.where(in_lanes, q_g, zero))
        dk[g] = dk_g
        dv[g] = dv_g
        return carry

    lax.fori_loop(0, groups, heads_of, 0)

    attended_t = att_t[...].astype(BF16)
    out_patch = (patched + mm(turned(attended_t).astype(BF16), wproj_ref[...])).astype(BF16)
    gw_ref[:, 3 * channels :] = mm(attended_t, upstream)
    dq_full = dq_t[...] * factor
    gw_ref[:, :channels] = mm(normed_t, turned(dq_full).astype(BF16))
    d_norm = mm(w_qkv[:, :channels], dq_full.astype(BF16))
    for part, ref in ((1, dk), (2, dv)):
        for g in range(groups):
            at = part * channels + g * group
            grads = ref[g]
            gw_ref[:, at : at + group] = mm(normed_t, grads.astype(BF16))
            d_norm = d_norm + mm(w_qkv[:, at : at + group], turned(grads).astype(BF16))
    d_layer = inverse * (
        d_norm
        - jnp.mean(d_norm, axis=0, keepdims=True)
        - centred_t * jnp.mean(d_norm * centred_t, axis=0, keepdims=True)
    )
    d_patch = (upstream.astype(F32) + turned(d_layer)).astype(BF16)
    key = jnp.broadcast_to(col[:, 0:1].astype(jnp.int32), (slots, length))
    back = one_hot(iota((slots, length), 1) == key)
    dp_ref[...] = mm(back, d_patch).astype(BF16)
    out_ref[...] = mm(back, out_patch).astype(BF16)


def patch(buf, w_qkv, w_proj, length):
    slots, channels = buf.shape[0], buf.shape[1] // 2
    group = 128
    groups = channels // group
    return pl.pallas_call(
        patch_kernel,
        out_shape=(
            jax.ShapeDtypeStruct((slots, channels), BF16),
            jax.ShapeDtypeStruct((slots, channels), BF16),
            jax.ShapeDtypeStruct((channels, 4 * channels), F32),
        ),
        in_specs=[VMEM_SPEC] * 3,
        out_specs=(VMEM_SPEC,) * 3,
        scratch_shapes=[pltpu.VMEM((groups, length, group), BF16)] * 4
        + [pltpu.VMEM((channels, length), BF16)] * 4
        + [pltpu.VMEM((channels, length), F32)] * 2
        + [pltpu.VMEM((groups, length, group), F32)] * 2,
        compiler_params=params(32),
        cost_estimate=cost(14e9, 4 << 20),
        name="patch",
    )(buf, w_qkv, w_proj)


def unpack(slot, buf):
    slots = buf.shape[0]
    length = slot.shape[1]
    wide = jnp.transpose(jnp.broadcast_to(slot[0:1, :], (128, length)), (1, 0))
    key = jnp.broadcast_to(wide[:, 0:1].astype(jnp.int32), (length, slots))
    return mm(one_hot(iota((length, slots), 1) == key), buf).astype(BF16)


def output_kernel(slot_ref, buf_ref, out_ref):
    out_ref[...] = unpack(slot_ref[...], buf_ref[...])


def return_rows(slot, buf):
    length, channels = slot.shape[1], buf.shape[1]
    return pl.pallas_call(
        output_kernel,
        out_shape=jax.ShapeDtypeStruct((length, channels), BF16),
        in_specs=[VMEM_SPEC] * 2,
        out_specs=VMEM_SPEC,
        compiler_params=params(12),
        cost_estimate=cost(2 * length * buf.shape[0] * channels, 1 << 20),
        name="return_rows",
    )(slot, buf)


PIECE = 128
PART = 16


def grad_kernel(sizes, slot_ref, buf_ref, g_ref, gw_ref, keep_ref, send_ref, d_mixed, total):
    step = pl.program_id(0)
    nz, nx, nc, nrep = sizes
    block = g_ref.shape[0]
    channels = buf_ref.shape[1]

    @pl.when(step == 0)
    def _():
        d_mixed[...] = unpack(slot_ref[...], buf_ref[...])

    total[pl.ds(pl.multiple_of(step * block, block), block), :] = mm(g_ref[...], d_mixed[...])

    @pl.when(step == pl.num_programs(0) - 1)
    def _():
        mine = (lax.axis_index("z"), lax.axis_index("x"), lax.axis_index("c"), lax.axis_index("rep"))
        rows = total.shape[0] // (nz * nx * nc)
        fine = gw_ref.shape[0] // (nz * nx * nc)
        for core in range(nc):
            for is_mine, ref in ((True, keep_ref), (False, send_ref)):
                same = mine[2] == core

                @pl.when(same if is_mine else jnp.logical_not(same))
                def _(core=core, ref=ref):
                    for z in range(nz):
                        sz = lax.rem(z - mine[0] + nz, nz)
                        for x in range(nx):
                            sx = lax.rem(x - mine[1] + nx, nx)
                            d = (z * nx + x) * nc + core
                            for part in range(PIECE // PART):
                                half, y = part // nrep, part % nrep
                                sy = lax.rem(y - mine[3] + nrep, nrep)
                                first = part * PART
                                if part == PIECE // PART - 1:
                                    terms = [
                                        gw_ref[
                                            d * fine : (d + 1) * fine,
                                            j * channels : (j + 1) * channels,
                                        ]
                                        for j in range(4)
                                    ]
                                    value = jnp.concatenate(terms, axis=0)
                                elif first + PART <= rows:
                                    value = total[d * rows + first : d * rows + first + PART, :]
                                else:
                                    left = rows - first
                                    value = jnp.concatenate(
                                        [
                                            total[d * rows + first : d * rows + rows, :],
                                            jnp.zeros((PART - left, channels), F32),
                                        ],
                                        axis=0,
                                    )
                                lead = sx * nrep + sy if half == 0 else sy * nx + sx
                                ref[half, lead, sz] = value.astype(BF16)


def grad_terms(slot, buf, g, gw, sizes):
    slots, channels = buf.shape
    length = slot.shape[1]
    nz, nx, _, nrep = sizes
    block = 3 * channels
    whole = lambda *shape: pl.BlockSpec(shape, lambda i: (0,) * len(shape))
    shape = (2, nx * nrep, nz, PART, channels)
    return pl.pallas_call(
        functools.partial(grad_kernel, sizes),
        grid=(g.shape[0] // block,),
        out_shape=(jax.ShapeDtypeStruct(shape, BF16), jax.ShapeDtypeStruct(shape, BF16)),
        in_specs=[
            whole(8, length),
            whole(slots, channels),
            pl.BlockSpec((block, length), lambda i: (i, 0)),
            whole(*gw.shape),
        ],
        out_specs=(whole(*shape), whole(*shape)),
        scratch_shapes=[
            pltpu.VMEM((length, channels), BF16),
            pltpu.VMEM((g.shape[0], channels), F32),
        ],
        compiler_params=params(32, dimension_semantics=("arbitrary",)),
        cost_estimate=cost(2 * g.shape[0] * length * channels, 12 << 20),
        name="grad_terms",
    )(slot, buf, in_hbm(g), gw)


def add_kernel(plan, *refs):
    count = sum(len(sources) for sources, _ in plan)
    ins, outs = refs[:count], refs[count:]
    at, to = 0, 0
    for sources, parts in plan:
        group = ins[at : at + len(sources)]
        at += len(sources)
        for part in range(parts):
            value = None
            for ref, (lead, per) in zip(group, sources):
                term = ref[lead + part * per : lead + (part + 1) * per].astype(F32)
                value = term if value is None else value + term
            outs[to][...] = value.astype(BF16)
            to += 1


def pair_kernel(sides, count, *refs):
    ins, outs = refs[: 2 * count], refs[2 * count :]
    for part, out in enumerate(outs):
        for side in range(sides):
            value = None
            for ref in ins[side * count : (side + 1) * count]:
                term = ref[part].astype(F32)
                value = term if value is None else value + term
            rows = value.shape[0]
            out[side * rows : (side + 1) * rows, :] = value.astype(BF16)


def add_pairs(a, b):
    parts, rows, channels = a[0].shape
    shape = jax.ShapeDtypeStruct((2 * rows, channels), BF16)
    return pl.pallas_call(
        functools.partial(pair_kernel, 2, len(a)),
        out_shape=(shape,) * parts,
        in_specs=[VMEM_SPEC] * (2 * len(a)),
        out_specs=(VMEM_SPEC,) * parts,
        compiler_params=params(8),
        cost_estimate=cost(1 << 20, 1 << 20),
        name="add_pairs",
    )(*a, *b)


def add_up(terms):
    plan, arrays, shapes = [], [], []
    for sources, lead_rows, parts in terms:
        per = lead_rows // parts
        plan.append((tuple((lead, per) for _, lead in sources), parts))
        arrays += [a for a, _ in sources]
        tail = sources[0][0].shape[1:]
        shapes += [jax.ShapeDtypeStruct((per, *tail), BF16)] * parts
    nbytes = sum(2 * s.size for s in shapes) * 3
    return pl.pallas_call(
        functools.partial(add_kernel, tuple(plan)),
        out_shape=tuple(shapes),
        in_specs=[VMEM_SPEC] * len(arrays),
        out_specs=(VMEM_SPEC,) * len(shapes),
        compiler_params=params(16),
        cost_estimate=cost(nbytes, nbytes),
        name="add_up",
    )(*arrays)


def final_kernel(sizes, *refs):
    _, _, _, nrep = sizes
    ins, (conv_ref, qkv_ref, proj_ref, piece) = refs[:nrep], refs[nrep:]
    me = lax.axis_index("rep")
    rows, channels = conv_ref.shape
    fine = qkv_ref.shape[0]
    for s, ref in enumerate(ins):
        y = lax.rem(me - s + nrep, nrep)
        for half in range(2):
            start = pl.multiple_of((half * nrep + y) * PART, PART)
            piece[pl.ds(start, PART), :] = ref[half * PART : (half + 1) * PART, :].astype(F32)
    conv_ref[...] = piece[:rows, :]
    base = PIECE - PART
    for j in range(3):
        qkv_ref[:, j * channels : (j + 1) * channels] = piece[base + fine * j : base + fine * (j + 1), :]
    proj_ref[...] = piece[base + 3 * fine : base + 4 * fine, :]


def shifted(a, axis, by):
    size = lax.axis_size(axis)
    return lax.ppermute(a, axis, [(i, (i + by) % size) for i in range(size)])


def per_device(features, neighbours, serial, w_conv, w_qkv, w_proj, cotangent):
    feats = features[0]
    length, channels = feats.shape
    slab_count = lax.axis_size(SPACE)
    sizes = tuple(lax.axis_size(a) for a in ("z", "x", "c", "rep"))
    nz, nx, _, nrep = sizes
    capacity = 2 * length // slab_count
    slots = slab_count * capacity
    up = [(i, i + 1) for i in range(slab_count - 1)]
    down = [(j, i) for i, j in up]

    def exchange(buf):
        parts = buf.reshape(slab_count, capacity, -1)
        out = lax.all_to_all(parts, SPACE, split_axis=0, concat_axis=0, tiled=True)
        return out.reshape(slots, -1)

    below = lax.ppermute(feats[length - RIM :], SPACE, up)
    above = lax.ppermute(feats[:RIM], SPACE, down)
    nb = jnp.transpose(neighbours, (2, 0, 1))
    g, row_buf, slot = gather_conv(
        serial, cotangent[0], nb, below, feats, above, w_conv, slots, capacity
    )
    out_buf, dp_buf, gw = patch(exchange(row_buf), w_qkv, w_proj, length)
    keep, send = grad_terms(slot, exchange(dp_buf), g, gw, sizes)

    got = lax.ppermute(send, "c", [(0, 1), (1, 0)])
    flat = lambda a: a.reshape(2 * nx * nrep, nz, PART, channels)
    keep, got = flat(keep), flat(got)
    half = nx * nrep
    parts = add_up([([(keep, 0), (got, 0)], half, nx), ([(keep, half), (got, half)], half, nrep)])
    *parts, out_buf = lax.optimization_barrier((*parts, out_buf))
    a, b = parts[:nx], parts[nx:]
    a_in = [shifted(a[s], "x", s) for s in range(1, nx)]
    b_in = [shifted(b[s], "rep", s) for s in range(1, nrep)]
    out_in = exchange(out_buf)
    output = return_rows(slot, out_in)
    parts = add_up(
        [
            ([(t, 0) for t in [a[0], *a_in]], nrep, nrep),
            ([(t, 0) for t in [b[0], *b_in]], nx, nx),
        ]
    )
    a, b = parts[:nrep], parts[nrep:]
    a_in = [shifted(a[s], "rep", s) for s in range(1, nrep)]
    b_in = [shifted(b[s], "x", s) for s in range(1, nx)]

    def rows_of(t):
        return t.reshape(nz, PART, channels)

    ab = add_pairs([rows_of(t) for t in (a[0], *a_in)], [rows_of(t) for t in (b[0], *b_in)])
    ab_in = [shifted(ab[s], "z", s) for s in range(1, nz)]
    (own,) = add_up([([(t, 0) for t in [ab[0], *ab_in]], 2 * PART, 1)])
    everyone = [own] + [shifted(own, "rep", s) for s in range(1, nrep)]
    places = slab_count
    g_conv, g_qkv, g_proj = pl.pallas_call(
        functools.partial(final_kernel, sizes),
        out_shape=(
            jax.ShapeDtypeStruct((w_conv.shape[0] // places, channels), F32),
            jax.ShapeDtypeStruct((channels // places, 3 * channels), F32),
            jax.ShapeDtypeStruct((channels // places, channels), F32),
        ),
        in_specs=[VMEM_SPEC] * nrep,
        out_specs=(VMEM_SPEC,) * 3,
        scratch_shapes=[pltpu.VMEM((PIECE, channels), F32)],
        compiler_params=params(8),
        name="final",
    )(*everyone)
    return (output[None], g_conv, g_qkv, g_proj)


def solution(mesh):
    fine = Mesh(mesh.devices.reshape(8, 4, 2, 4), ("z", "x", "c", "rep"))

    return jax.shard_map(
        per_device,
        mesh=fine,
        in_specs=(
            P("rep", SPACE, None),
            P("rep", SPACE, None),
            P("rep", SPACE),
            P(),
            P(),
            P(),
            P("rep", SPACE, None),
        ),
        out_specs=(P("rep", SPACE, None), P(SPACE, None), P(SPACE, None), P(SPACE, None)),
        check_vma=False,
    )
```

profile of v0, /device:TPU:32, one launch (start us, length us, event | category | flops | bytes accessed | tf_op | source)
XLA Modules:
  0.0 194.5 jit_solution(1550603967001262968)
XLA Ops:
  0.6 0.9 slice_bitcast_fusion
  1.5 3.7 %collective-permute-start.1 = (bf16[128,256]{1,0:T(8,128)(2,1)S(1)}, bf16[128,256]{1,0:T(8,128)(2,1)S(1)}, u32[]{:S(2)}, u32[]{:S(2)}) collective-permute-start(bf16[128,256]{1,0:T(8,128)(2,1)S(1)} %get-tuple-element.92), channel_id=1, source_target_pairs={{4,0},{8,4},{12,8},{16,12},{20,16},{24,20},{28,24},{32,28},{36,32}... | collective-permute-start | bytes 196616 | tf_op jit(solution)/shard_map/ppermute | solution.py:505
  5.2 1.9 collective-permute-start
  7.1 0.0 collective-permute-done.1.above_ref
  7.1 5.8 %collective-permute-done.below_ref = bf16[128,256]{1,0:T(8,128)(2,1)S(1)} collective-permute-done((bf16[128,256]{1,0:T(8,128)(2,1)S(1)}, bf16[128,256]{1,0:T(8,128)(2,1)S(1)}, u32[]{:S(2)}, u32[]{:S(2)}) %collective-permute-start) | collective-permute-done | bytes 65568 | tf_op jit(solution)/shard_map/ppermute | solution.py:504
  12.9 16.3 %gather_conv.1 = (bf16[6912,512]{1,0:T(8,128)(2,1)}, bf16[1024,512]{1,0:T(8,128)(2,1)S(1)}, f32[8,512]{1,0:T(8,128)S(1)}) custom-call(s32[1,512]{1,0:T(1,128)} %serial_ref.1, bf16[512,256]{1,0:T(8,128)(2,1)} %bitcast.42, s32[27,1,512]{2,1,0:T(1,128)} %bitcast.43, bf16[128,256]{1,0:T(8,128)(2,1)S(1)} %collective-permute-done.below_ref, ...), custom_call_target="tpu_custom_call" | custom-call | flops 7247757312 | bytes 12582912 | tf_op jit(solution)/shard_map/gather_conv/pallas_call | solution.py:132
  29.2 38.2 %all_to_all.15 = bf16[64,16,512]{2,1,0:T(8,128)(2,1)S(1)} all-to-all(bf16[64,16,512]{2,1,0:T(8,128)(2,1)S(1)} %bitcast.29), channel_id=1, replica_groups=mesh['z'=8,'x'=4,'c'=2,'rep'=4] {'z','x','c'}, dimensions={0} | all-to-all | bytes 2097152 | tf_op jit(solution)/shard_map/all_to_all | solution.py:501
  67.4 0.0 copy-done.1
  67.4 15.7 %patch.1 = (bf16[1024,256]{1,0:T(8,128)(2,1)}, bf16[1024,256]{1,0:T(8,128)(2,1)S(1)}, f32[256,1024]{1,0:T(8,128)S(1)}) custom-call(bf16[1024,512]{1,0:T(8,128)(2,1)S(1)} %bitcast.30, bf16[256,768]{1,0:T(8,128)(2,1)S(1)} %copy-done, bf16[256,256]{1,0:T(8,128)(2,1)S(1)} %copy-done.1), custom_call_target="tpu_custom_call" | custom-call | flops 14000000000 | bytes 4194304 | tf_op jit(solution)/shard_map/patch/pallas_call | solution.py:271
  83.1 23.0 %all_to_all.16 = bf16[64,16,256]{2,1,0:T(8,128)(2,1)S(1)} all-to-all(bf16[64,16,256]{2,1,0:T(8,128)(2,1)S(1)} %bitcast.32), channel_id=1, replica_groups=mesh['z'=8,'x'=4,'c'=2,'rep'=4] {'z','x','c'}, dimensions={0} | all-to-all | bytes 1048576 | tf_op jit(solution)/shard_map/all_to_all | solution.py:501
  106.1 9.3 %grad_terms.1 = (bf16[2,16,8,16,256]{4,3,2,1,0:T(8,128)(2,1)S(1)}, bf16[2,16,8,16,256]{4,3,2,1,0:T(8,128)(2,1)S(1)}) custom-call(f32[8,512]{1,0:T(8,128)S(1)} %get-tuple-element.48.slot_ref, bf16[1024,256]{1,0:T(8,128)(2,1)S(1)} %bitcast.28, bf16[6912,512]{1,0:T(8,128)(2,1)} %get-tuple-element.51.g_ref, f32[256,1024]{1,0:T(8,128)S(1)} %get-tuple-element.52.gw_ref), custom_call_target="tpu_custom_call" | custom-call | flops 1811939328 | bytes 12582912 | tf_op jit(solution)/shard_map/grad_terms/pallas_call | solution.py:382
  115.4 0.6 collective-permute-start.2
  115.9 3.8 %collective-permute-done.2 = bf16[2,16,8,16,256]{4,3,2,1,0:T(8,128)(2,1)S(1)} collective-permute-done((bf16[2,16,8,16,256]{4,3,2,1,0:T(8,128)(2,1)S(1)}, bf16[2,16,8,16,256]{4,3,2,1,0:T(8,128)(2,1)S(1)}, u32[]{:S(2)}, u32[]{:S(2)}) %collective-permute-start.2) | collective-permute-done | bytes 2097184 | tf_op jit(solution)/shard_map/ppermute | solution.py:513
  119.7 0.5 add_up.3
  120.2 6.6 %all-to-all-start.2 = ((bf16[64,16,256]{2,1,0:T(8,128)(2,1)}), bf16[64,16,256]{2,1,0:T(8,128)(2,1)S(1)}, u32[]{:S(2)}, u32[]{:S(2)}) async-start(bf16[64,16,256]{2,1,0:T(8,128)(2,1)} %bitcast.11), calls=%async_computation.2 | async-start | bytes 1048576 | tf_op jit(solution)/shard_map/all_to_all | solution.py:501
  126.8 1.5 collective-permute-start.3
  128.3 2.7 %collective-permute-start.4 = (bf16[4,8,16,256]{3,2,1,0:T(8,128)(2,1)S(1)}, bf16[4,8,16,256]{3,2,1,0:T(8,128)(2,1)S(1)}, u32[]{:S(2)}, u32[]{:S(2)}) collective-permute-start(bf16[4,8,16,256]{3,2,1,0:T(8,128)(2,1)S(1)} %get-tuple-element.67), channel_id=1, source_target_pairs={{0,16},{8,24},{16,0},{24,8},{1,17},{9,25},{17,1},{25,9},{2,18},{10... | collective-permute-start | bytes 786440 | tf_op jit(solution)/shard_map/ppermute | solution.py:485
  131.0 1.5 collective-permute-start.5
  132.5 1.6 collective-permute-start.6
  134.1 2.9 %collective-permute-start.7 = (bf16[4,8,16,256]{3,2,1,0:T(8,128)(2,1)S(1)}, bf16[4,8,16,256]{3,2,1,0:T(8,128)(2,1)S(1)}, u32[]{:S(2)}, u32[]{:S(2)}) collective-permute-start(bf16[4,8,16,256]{3,2,1,0:T(8,128)(2,1)S(1)} %get-tuple-element.71), channel_id=1, source_target_pairs={{0,2},{1,3},{2,0},{3,1},{4,6},{5,7},{6,4},{7,5},{8,10},{9,11},{10,... | collective-permute-start | bytes 786440 | tf_op jit(solution)/shard_map/ppermute | solution.py:485
  137.0 5.0 %collective-permute-done.3.refs_1_ = bf16[4,8,16,256]{3,2,1,0:T(8,128)(2,1)S(1)} collective-permute-done((bf16[4,8,16,256]{3,2,1,0:T(8,128)(2,1)S(1)}, bf16[4,8,16,256]{3,2,1,0:T(8,128)(2,1)S(1)}, u32[]{:S(2)}, u32[]{:S(2)}) %collective-permute-start.3) | collective-permute-done | bytes 262176 | tf_op jit(solution)/shard_map/ppermute | solution.py:485
  142.0 3.0 %collective-permute-start.8 = (bf16[4,8,16,256]{3,2,1,0:T(8,128)(2,1)S(1)}, bf16[4,8,16,256]{3,2,1,0:T(8,128)(2,1)S(1)}, u32[]{:S(2)}, u32[]{:S(2)}) collective-permute-start(bf16[4,8,16,256]{3,2,1,0:T(8,128)(2,1)S(1)} %get-tuple-element.72), channel_id=1, source_target_pairs={{0,3},{1,0},{2,1},{3,2},{4,7},{5,4},{6,5},{7,6},{8,11},{9,8},{10,9... | collective-permute-start | bytes 786440 | tf_op jit(solution)/shard_map/ppermute | solution.py:485
  145.0 2.6 %collective-permute-done.4.refs_2_ = bf16[4,8,16,256]{3,2,1,0:T(8,128)(2,1)S(1)} collective-permute-done((bf16[4,8,16,256]{3,2,1,0:T(8,128)(2,1)S(1)}, bf16[4,8,16,256]{3,2,1,0:T(8,128)(2,1)S(1)}, u32[]{:S(2)}, u32[]{:S(2)}) %collective-permute-start.4) | collective-permute-done | bytes 262176 | tf_op jit(solution)/shard_map/ppermute | solution.py:485
  147.6 0.0 collective-permute-done.5.refs_3_
  147.6 0.0 collective-permute-done.6.refs_5_
  147.6 0.4 collective-permute-done.7.refs_6_
  148.0 1.3 collective-permute-done.8.refs_7_
  149.3 0.3 add_up.4
  149.6 1.1 collective-permute-start.9
  150.7 4.1 %collective-permute-start.10 = (bf16[1,8,16,256]{3,2,1,0:T(8,128)(2,1)S(1)}, bf16[1,8,16,256]{3,2,1,0:T(8,128)(2,1)S(1)}, u32[]{:S(2)}, u32[]{:S(2)}) collective-permute-start(bf16[1,8,16,256]{3,2,1,0:T(8,128)(2,1)S(1)} %get-tuple-element.75), channel_id=1, source_target_pairs={{0,2},{1,3},{2,0},{3,1},{4,6},{5,7},{6,4},{7,5},{8,10},{9,11},{10,... | collective-permute-start | bytes 196616 | tf_op jit(solution)/shard_map/ppermute | solution.py:485
  154.8 0.1 collective-permute-start.11
  155.0 0.2 collective-permute-start.12
  155.2 6.7 %collective-permute-start.13 = (bf16[1,8,16,256]{3,2,1,0:T(8,128)(2,1)S(1)}, bf16[1,8,16,256]{3,2,1,0:T(8,128)(2,1)S(1)}, u32[]{:S(2)}, u32[]{:S(2)}) collective-permute-start(bf16[1,8,16,256]{3,2,1,0:T(8,128)(2,1)S(1)} %get-tuple-element.79), channel_id=1, source_target_pairs={{0,16},{8,24},{16,0},{24,8},{1,17},{9,25},{17,1},{25,9},{2,18},{10... | collective-permute-start | bytes 196616 | tf_op jit(solution)/shard_map/ppermute | solution.py:485
  161.9 0.0 collective-permute-done.9
  161.9 2.6 %collective-permute-start.14 = (bf16[1,8,16,256]{3,2,1,0:T(8,128)(2,1)S(1)}, bf16[1,8,16,256]{3,2,1,0:T(8,128)(2,1)S(1)}, u32[]{:S(2)}, u32[]{:S(2)}) collective-permute-start(bf16[1,8,16,256]{3,2,1,0:T(8,128)(2,1)S(1)} %get-tuple-element.80), channel_id=1, source_target_pairs={{0,24},{8,0},{16,8},{24,16},{1,25},{9,1},{17,9},{25,17},{2,26},{10... | collective-permute-start | bytes 196616 | tf_op jit(solution)/shard_map/ppermute | solution.py:485
  164.6 0.0 collective-permute-done.10
  164.6 0.0 collective-permute-done.11
  164.6 0.0 collective-permute-done.12
  164.6 0.3 collective-permute-done.13
  164.9 1.6 collective-permute-done.14
  166.5 0.1 add_pairs.1
  166.5 0.1 collective-permute-start.15
  166.6 5.0 %collective-permute-start.16 = (bf16[32,256]{1,0:T(8,128)(2,1)S(1)}, bf16[32,256]{1,0:T(8,128)(2,1)S(1)}, u32[]{:S(2)}, u32[]{:S(2)}) collective-permute-start(bf16[32,256]{1,0:T(8,128)(2,1)S(1)} %get-tuple-element.83), channel_id=1, source_target_pairs={{0,64},{32,96},{64,128},{96,160},{128,192},{160,224},{192,0},{224,... | collective-permute-start | bytes 49160 | tf_op jit(solution)/shard_map/ppermute | solution.py:485
  171.6 0.9 collective-permute-start.17
  172.6 0.6 collective-permute-start.18
  173.1 4.0 %collective-permute-start.19 = (bf16[32,256]{1,0:T(8,128)(2,1)S(1)}, bf16[32,256]{1,0:T(8,128)(2,1)S(1)}, u32[]{:S(2)}, u32[]{:S(2)}) collective-permute-start(bf16[32,256]{1,0:T(8,128)(2,1)S(1)} %get-tuple-element.86), channel_id=1, source_target_pairs={{0,160},{32,192},{64,224},{96,0},{128,32},{160,64},{192,96},{224,1... | collective-permute-start | bytes 49160 | tf_op jit(solution)/shard_map/ppermute | solution.py:485
  177.1 0.0 collective-permute-done.15.refs_1_
  177.1 1.9 collective-permute-start.20
  179.0 0.0 collective-permute-done.16.refs_2_
  179.0 2.8 %collective-permute-start.21 = (bf16[32,256]{1,0:T(8,128)(2,1)S(1)}, bf16[32,256]{1,0:T(8,128)(2,1)S(1)}, u32[]{:S(2)}, u32[]{:S(2)}) collective-permute-start(bf16[32,256]{1,0:T(8,128)(2,1)S(1)} %get-tuple-element.88), channel_id=1, source_target_pairs={{0,224},{32,0},{64,32},{96,64},{128,96},{160,128},{192,160},{224,1... | collective-permute-start | bytes 49160 | tf_op jit(solution)/shard_map/ppermute | solution.py:485
  181.8 0.0 collective-permute-done.17.refs_3_
  181.8 0.0 collective-permute-done.18.refs_4_
  181.8 0.0 collective-permute-done.19.refs_5_
  181.8 0.0 collective-permute-done.20.refs_6_
  181.8 1.4 collective-permute-done.21.refs_7_
  183.3 0.6 collective-permute-start.24
  183.9 3.5 %collective-permute-start.23 = (bf16[32,256]{1,0:T(8,128)(2,1)S(1)}, bf16[32,256]{1,0:T(8,128)(2,1)S(1)}, u32[]{:S(2)}, u32[]{:S(2)}) collective-permute-start(bf16[32,256]{1,0:T(8,128)(2,1)S(1)} %add_up.5.refs_0_), channel_id=1, source_target_pairs={{0,2},{1,3},{2,0},{3,1},{4,6},{5,7},{6,4},{7,5},{8,10},{9,11},{10,... | collective-permute-start | bytes 49160 | tf_op jit(solution)/shard_map/ppermute | solution.py:485
  187.4 0.0 collective-permute-start.22
  187.4 0.0 collective-permute-done.24.refs_3_
  187.4 1.7 collective-permute-done.23.refs_2_
  189.1 3.2 %collective-permute-done.22.refs_1_ = bf16[32,256]{1,0:T(8,128)(2,1)S(1)} collective-permute-done((bf16[32,256]{1,0:T(8,128)(2,1)S(1)}, bf16[32,256]{1,0:T(8,128)(2,1)S(1)}, u32[]{:S(2)}, u32[]{:S(2)}) %collective-permute-start.22) | collective-permute-done | bytes 16416 | tf_op jit(solution)/shard_map/ppermute | solution.py:485
  192.4 0.7 final.1
  193.0 0.0 all-to-all-done.2
  193.1 1.4 return_rows.1
  (4 shorter events, 0.0 us)
Async XLA Ops:
  1.5 5.6 %collective-permute-start.1 = (bf16[128,256]{1,0:T(8,128)(2,1)S(1)}, bf16[128,256]{1,0:T(8,128)(2,1)S(1)}, u32[]{:S(2)}, u32[]{:S(2)}) collective-permute-start(bf16[128,256]{1,0:T(8,128)(2,1)S(1)} %get-tuple-element.92), channel_id=1, source_target_pairs={{4,0},{8,4},{12,8},{16,12},{20,16},{24,20},{28,24},{32,28},{36,32}... | collective-permute-start | bytes 196616 | tf_op jit(solution)/shard_map/ppermute | solution.py:505
  5.2 7.7 %collective-permute-start = (bf16[128,256]{1,0:T(8,128)(2,1)S(1)}, bf16[128,256]{1,0:T(8,128)(2,1)S(1)}, u32[]{:S(2)}, u32[]{:S(2)}) collective-permute-start(bf16[128,256]{1,0:T(8,128)(2,1)S(1)} %get-tuple-element.93), channel_id=1, source_target_pairs={{0,4},{4,8},{8,12},{12,16},{16,20},{20,24},{24,28},{28,32},{32,36}... | collective-permute-start | bytes 196616 | tf_op jit(solution)/shard_map/ppermute | solution.py:504
  29.2 38.2 %copy-start = (bf16[256,768]{1,0:T(8,128)(2,1)S(1)}, bf16[256,768]{1,0:T(8,128)(2,1)}, u32[]{:S(2)}) copy-start(bf16[256,768]{1,0:T(8,128)(2,1)} %wqkv_ref.1) | copy-start | bytes 1179652
  29.2 38.2 %copy-start.1 = (bf16[256,256]{1,0:T(8,128)(2,1)S(1)}, bf16[256,256]{1,0:T(8,128)(2,1)}, u32[]{:S(2)}) copy-start(bf16[256,256]{1,0:T(8,128)(2,1)} %wproj_ref.1) | copy-start | bytes 393220
  115.4 4.4 %collective-permute-start.2 = (bf16[2,16,8,16,256]{4,3,2,1,0:T(8,128)(2,1)S(1)}, bf16[2,16,8,16,256]{4,3,2,1,0:T(8,128)(2,1)S(1)}, u32[]{:S(2)}, u32[]{:S(2)}) collective-permute-start(bf16[2,16,8,16,256]{4,3,2,1,0:T(8,128)(2,1)S(1)} %get-tuple-element.54), channel_id=1, source_target_pairs={{0,4},{4,0},{1,5},{5,1},{2,6},{6,2},{3,7},{7,3},{8,12},{12,8},{9,1... | collective-permute-start | bytes 6291464 | tf_op jit(solution)/shard_map/ppermute | solution.py:513
  120.2 72.9 %all-to-all-start.2 = ((bf16[64,16,256]{2,1,0:T(8,128)(2,1)}), bf16[64,16,256]{2,1,0:T(8,128)(2,1)S(1)}, u32[]{:S(2)}, u32[]{:S(2)}) async-start(bf16[64,16,256]{2,1,0:T(8,128)(2,1)} %bitcast.11), calls=%async_computation.2 | async-start | bytes 1048576 | tf_op jit(solution)/shard_map/all_to_all | solution.py:501
  126.8 15.2 %collective-permute-start.3 = (bf16[4,8,16,256]{3,2,1,0:T(8,128)(2,1)S(1)}, bf16[4,8,16,256]{3,2,1,0:T(8,128)(2,1)S(1)}, u32[]{:S(2)}, u32[]{:S(2)}) collective-permute-start(bf16[4,8,16,256]{3,2,1,0:T(8,128)(2,1)S(1)} %get-tuple-element.66), channel_id=1, source_target_pairs={{0,8},{8,16},{16,24},{24,0},{1,9},{9,17},{17,25},{25,1},{2,10},{10... | collective-permute-start | bytes 786440 | tf_op jit(solution)/shard_map/ppermute | solution.py:485
  128.3 19.3 %collective-permute-start.4 = (bf16[4,8,16,256]{3,2,1,0:T(8,128)(2,1)S(1)}, bf16[4,8,16,256]{3,2,1,0:T(8,128)(2,1)S(1)}, u32[]{:S(2)}, u32[]{:S(2)}) collective-permute-start(bf16[4,8,16,256]{3,2,1,0:T(8,128)(2,1)S(1)} %get-tuple-element.67), channel_id=1, source_target_pairs={{0,16},{8,24},{16,0},{24,8},{1,17},{9,25},{17,1},{25,9},{2,18},{10... | collective-permute-start | bytes 786440 | tf_op jit(solution)/shard_map/ppermute | solution.py:485
  131.0 16.6 %collective-permute-start.5 = (bf16[4,8,16,256]{3,2,1,0:T(8,128)(2,1)S(1)}, bf16[4,8,16,256]{3,2,1,0:T(8,128)(2,1)S(1)}, u32[]{:S(2)}, u32[]{:S(2)}) collective-permute-start(bf16[4,8,16,256]{3,2,1,0:T(8,128)(2,1)S(1)} %get-tuple-element.68), channel_id=1, source_target_pairs={{0,24},{8,0},{16,8},{24,16},{1,25},{9,1},{17,9},{25,17},{2,26},{10... | collective-permute-start | bytes 786440 | tf_op jit(solution)/shard_map/ppermute | solution.py:485
  132.5 15.1 %collective-permute-start.6 = (bf16[4,8,16,256]{3,2,1,0:T(8,128)(2,1)S(1)}, bf16[4,8,16,256]{3,2,1,0:T(8,128)(2,1)S(1)}, u32[]{:S(2)}, u32[]{:S(2)}) collective-permute-start(bf16[4,8,16,256]{3,2,1,0:T(8,128)(2,1)S(1)} %get-tuple-element.70), channel_id=1, source_target_pairs={{0,1},{1,2},{2,3},{3,0},{4,5},{5,6},{6,7},{7,4},{8,9},{9,10},{10,1... | collective-permute-start | bytes 786440 | tf_op jit(solution)/shard_map/ppermute | solution.py:485
  134.1 14.0 %collective-permute-start.7 = (bf16[4,8,16,256]{3,2,1,0:T(8,128)(2,1)S(1)}, bf16[4,8,16,256]{3,2,1,0:T(8,128)(2,1)S(1)}, u32[]{:S(2)}, u32[]{:S(2)}) collective-permute-start(bf16[4,8,16,256]{3,2,1,0:T(8,128)(2,1)S(1)} %get-tuple-element.71), channel_id=1, source_target_pairs={{0,2},{1,3},{2,0},{3,1},{4,6},{5,7},{6,4},{7,5},{8,10},{9,11},{10,... | collective-permute-start | bytes 786440 | tf_op jit(solution)/shard_map/ppermute | solution.py:485
  142.0 7.4 %collective-permute-start.8 = (bf16[4,8,16,256]{3,2,1,0:T(8,128)(2,1)S(1)}, bf16[4,8,16,256]{3,2,1,0:T(8,128)(2,1)S(1)}, u32[]{:S(2)}, u32[]{:S(2)}) collective-permute-start(bf16[4,8,16,256]{3,2,1,0:T(8,128)(2,1)S(1)} %get-tuple-element.72), channel_id=1, source_target_pairs={{0,3},{1,0},{2,1},{3,2},{4,7},{5,4},{6,5},{7,6},{8,11},{9,8},{10,9... | collective-permute-start | bytes 786440 | tf_op jit(solution)/shard_map/ppermute | solution.py:485
  149.6 12.3 %collective-permute-start.9 = (bf16[1,8,16,256]{3,2,1,0:T(8,128)(2,1)S(1)}, bf16[1,8,16,256]{3,2,1,0:T(8,128)(2,1)S(1)}, u32[]{:S(2)}, u32[]{:S(2)}) collective-permute-start(bf16[1,8,16,256]{3,2,1,0:T(8,128)(2,1)S(1)} %get-tuple-element.74), channel_id=1, source_target_pairs={{0,1},{1,2},{2,3},{3,0},{4,5},{5,6},{6,7},{7,4},{8,9},{9,10},{10,1... | collective-permute-start | bytes 196616 | tf_op jit(solution)/shard_map/ppermute | solution.py:485
  150.7 13.8 %collective-permute-start.10 = (bf16[1,8,16,256]{3,2,1,0:T(8,128)(2,1)S(1)}, bf16[1,8,16,256]{3,2,1,0:T(8,128)(2,1)S(1)}, u32[]{:S(2)}, u32[]{:S(2)}) collective-permute-start(bf16[1,8,16,256]{3,2,1,0:T(8,128)(2,1)S(1)} %get-tuple-element.75), channel_id=1, source_target_pairs={{0,2},{1,3},{2,0},{3,1},{4,6},{5,7},{6,4},{7,5},{8,10},{9,11},{10,... | collective-permute-start | bytes 196616 | tf_op jit(solution)/shard_map/ppermute | solution.py:485
  154.8 9.7 %collective-permute-start.11 = (bf16[1,8,16,256]{3,2,1,0:T(8,128)(2,1)S(1)}, bf16[1,8,16,256]{3,2,1,0:T(8,128)(2,1)S(1)}, u32[]{:S(2)}, u32[]{:S(2)}) collective-permute-start(bf16[1,8,16,256]{3,2,1,0:T(8,128)(2,1)S(1)} %get-tuple-element.76), channel_id=1, source_target_pairs={{0,3},{1,0},{2,1},{3,2},{4,7},{5,4},{6,5},{7,6},{8,11},{9,8},{10,9... | collective-permute-start | bytes 196616 | tf_op jit(solution)/shard_map/ppermute | solution.py:485
  155.0 9.6 %collective-permute-start.12 = (bf16[1,8,16,256]{3,2,1,0:T(8,128)(2,1)S(1)}, bf16[1,8,16,256]{3,2,1,0:T(8,128)(2,1)S(1)}, u32[]{:S(2)}, u32[]{:S(2)}) collective-permute-start(bf16[1,8,16,256]{3,2,1,0:T(8,128)(2,1)S(1)} %get-tuple-element.78), channel_id=1, source_target_pairs={{0,8},{8,16},{16,24},{24,0},{1,9},{9,17},{17,25},{25,1},{2,10},{10... | collective-permute-start | bytes 196616 | tf_op jit(solution)/shard_map/ppermute | solution.py:485
  155.2 9.7 %collective-permute-start.13 = (bf16[1,8,16,256]{3,2,1,0:T(8,128)(2,1)S(1)}, bf16[1,8,16,256]{3,2,1,0:T(8,128)(2,1)S(1)}, u32[]{:S(2)}, u32[]{:S(2)}) collective-permute-start(bf16[1,8,16,256]{3,2,1,0:T(8,128)(2,1)S(1)} %get-tuple-element.79), channel_id=1, source_target_pairs={{0,16},{8,24},{16,0},{24,8},{1,17},{9,25},{17,1},{25,9},{2,18},{10... | collective-permute-start | bytes 196616 | tf_op jit(solution)/shard_map/ppermute | solution.py:485
  161.9 4.5 %collective-permute-start.14 = (bf16[1,8,16,256]{3,2,1,0:T(8,128)(2,1)S(1)}, bf16[1,8,16,256]{3,2,1,0:T(8,128)(2,1)S(1)}, u32[]{:S(2)}, u32[]{:S(2)}) collective-permute-start(bf16[1,8,16,256]{3,2,1,0:T(8,128)(2,1)S(1)} %get-tuple-element.80), channel_id=1, source_target_pairs={{0,24},{8,0},{16,8},{24,16},{1,25},{9,1},{17,9},{25,17},{2,26},{10... | collective-permute-start | bytes 196616 | tf_op jit(solution)/shard_map/ppermute | solution.py:485
  166.5 10.6 %collective-permute-start.15 = (bf16[32,256]{1,0:T(8,128)(2,1)S(1)}, bf16[32,256]{1,0:T(8,128)(2,1)S(1)}, u32[]{:S(2)}, u32[]{:S(2)}) collective-permute-start(bf16[32,256]{1,0:T(8,128)(2,1)S(1)} %get-tuple-element.82), channel_id=1, source_target_pairs={{0,32},{32,64},{64,96},{96,128},{128,160},{160,192},{192,224},{224... | collective-permute-start | bytes 49160 | tf_op jit(solution)/shard_map/ppermute | solution.py:485
  166.6 12.4 %collective-permute-start.16 = (bf16[32,256]{1,0:T(8,128)(2,1)S(1)}, bf16[32,256]{1,0:T(8,128)(2,1)S(1)}, u32[]{:S(2)}, u32[]{:S(2)}) collective-permute-start(bf16[32,256]{1,0:T(8,128)(2,1)S(1)} %get-tuple-element.83), channel_id=1, source_target_pairs={{0,64},{32,96},{64,128},{96,160},{128,192},{160,224},{192,0},{224,... | collective-permute-start | bytes 49160 | tf_op jit(solution)/shard_map/ppermute | solution.py:485
  171.6 10.2 %collective-permute-start.17 = (bf16[32,256]{1,0:T(8,128)(2,1)S(1)}, bf16[32,256]{1,0:T(8,128)(2,1)S(1)}, u32[]{:S(2)}, u32[]{:S(2)}) collective-permute-start(bf16[32,256]{1,0:T(8,128)(2,1)S(1)} %get-tuple-element.84), channel_id=1, source_target_pairs={{0,96},{32,128},{64,160},{96,192},{128,224},{160,0},{192,32},{224,... | collective-permute-start | bytes 49160 | tf_op jit(solution)/shard_map/ppermute | solution.py:485
  172.6 9.2 %collective-permute-start.18 = (bf16[32,256]{1,0:T(8,128)(2,1)S(1)}, bf16[32,256]{1,0:T(8,128)(2,1)S(1)}, u32[]{:S(2)}, u32[]{:S(2)}) collective-permute-start(bf16[32,256]{1,0:T(8,128)(2,1)S(1)} %get-tuple-element.85), channel_id=1, source_target_pairs={{0,128},{32,160},{64,192},{96,224},{128,0},{160,32},{192,64},{224,... | collective-permute-start | bytes 49160 | tf_op jit(solution)/shard_map/ppermute | solution.py:485
  173.1 8.7 %collective-permute-start.19 = (bf16[32,256]{1,0:T(8,128)(2,1)S(1)}, bf16[32,256]{1,0:T(8,128)(2,1)S(1)}, u32[]{:S(2)}, u32[]{:S(2)}) collective-permute-start(bf16[32,256]{1,0:T(8,128)(2,1)S(1)} %get-tuple-element.86), channel_id=1, source_target_pairs={{0,160},{32,192},{64,224},{96,0},{128,32},{160,64},{192,96},{224,1... | collective-permute-start | bytes 49160 | tf_op jit(solution)/shard_map/ppermute | solution.py:485
  177.1 4.7 %collective-permute-start.20 = (bf16[32,256]{1,0:T(8,128)(2,1)S(1)}, bf16[32,256]{1,0:T(8,128)(2,1)S(1)}, u32[]{:S(2)}, u32[]{:S(2)}) collective-permute-start(bf16[32,256]{1,0:T(8,128)(2,1)S(1)} %get-tuple-element.87), channel_id=1, source_target_pairs={{0,192},{32,224},{64,0},{96,32},{128,64},{160,96},{192,128},{224,1... | collective-permute-start | bytes 49160 | tf_op jit(solution)/shard_map/ppermute | solution.py:485
  179.0 4.2 %collective-permute-start.21 = (bf16[32,256]{1,0:T(8,128)(2,1)S(1)}, bf16[32,256]{1,0:T(8,128)(2,1)S(1)}, u32[]{:S(2)}, u32[]{:S(2)}) collective-permute-start(bf16[32,256]{1,0:T(8,128)(2,1)S(1)} %get-tuple-element.88), channel_id=1, source_target_pairs={{0,224},{32,0},{64,32},{96,64},{128,96},{160,128},{192,160},{224,1... | collective-permute-start | bytes 49160 | tf_op jit(solution)/shard_map/ppermute | solution.py:485
  183.3 4.2 %collective-permute-start.24 = (bf16[32,256]{1,0:T(8,128)(2,1)S(1)}, bf16[32,256]{1,0:T(8,128)(2,1)S(1)}, u32[]{:S(2)}, u32[]{:S(2)}) collective-permute-start(bf16[32,256]{1,0:T(8,128)(2,1)S(1)} %add_up.5.refs_0_), channel_id=1, source_target_pairs={{0,3},{1,0},{2,1},{3,2},{4,7},{5,4},{6,5},{7,6},{8,11},{9,8},{10,9... | collective-permute-start | bytes 49160 | tf_op jit(solution)/shard_map/ppermute | solution.py:485
  183.9 5.2 %collective-permute-start.23 = (bf16[32,256]{1,0:T(8,128)(2,1)S(1)}, bf16[32,256]{1,0:T(8,128)(2,1)S(1)}, u32[]{:S(2)}, u32[]{:S(2)}) collective-permute-start(bf16[32,256]{1,0:T(8,128)(2,1)S(1)} %add_up.5.refs_0_), channel_id=1, source_target_pairs={{0,2},{1,3},{2,0},{3,1},{4,6},{5,7},{6,4},{7,5},{8,10},{9,11},{10,... | collective-permute-start | bytes 49160 | tf_op jit(solution)/shard_map/ppermute | solution.py:485
  187.4 4.9 %collective-permute-start.22 = (bf16[32,256]{1,0:T(8,128)(2,1)S(1)}, bf16[32,256]{1,0:T(8,128)(2,1)S(1)}, u32[]{:S(2)}, u32[]{:S(2)}) collective-permute-start(bf16[32,256]{1,0:T(8,128)(2,1)S(1)} %add_up.5.refs_0_), channel_id=1, source_target_pairs={{0,1},{1,2},{2,3},{3,0},{4,5},{5,6},{6,7},{7,4},{8,9},{9,10},{10,1... | collective-permute-start | bytes 49160 | tf_op jit(solution)/shard_map/ppermute | solution.py:485
where the time goes:
time: 198 us; the launch traced here: 194 us
  blocking collectives  61.2 us (31%)
  starting transfers between devices  60.3 us (30%)
  Pallas kernels  44.2 us (22%)
  waiting for transfers between devices  27.2 us (14%)
    all_to_all x2, blocking collectives, exchange(): out = lax.all_to_all(parts, SPACE, split_axis=0, concat_axis=0, tiled=True)  61.2 us
    ppermute x22, starting transfers between devices, shifted(): return lax.ppermute(a, axis, [(i, (i + by) % size) for i in range(size)])  47.5 us
    ppermute x22, waiting for transfers between devices, shifted(): return lax.ppermute(a, axis, [(i, (i + by) % size) for i in range(size)])  17.6 us
    pallas_call x1, Pallas kernels, gather_conv(): pl.pallas_call(functools.partial(conv_kernel, capacity), grid=(count // p...  16.3 us
    pallas_call x1, Pallas kernels, patch(): pl.pallas_call(patch_kernel, out_shape=(jax.ShapeDtypeStruct((slots, chan...  15.7 us
    pallas_call x1, Pallas kernels, grad_terms(): pl.pallas_call(functools.partial(grad_kernel, sizes), grid=(g.shape[0] //...  9.26 us
    all_to_all x1, starting transfers between devices, exchange(): out = lax.all_to_all(parts, SPACE, split_axis=0, concat_axis=0, tiled=True)  6.61 us
    ppermute x1, waiting for transfers between devices, per_device(): below = lax.ppermute(feats[length - RIM:], SPACE, up)  5.76 us
  transfers between devices with their start and end apart: 26, of which 11 were waited for; matrix products, arithmetic and copies ran while one was open for 0% of the time, Pallas kernels for 1%

commit v1 on v0

--- a/solution.py
+++ b/solution.py
@@ -69,22 +69,57 @@
     return jnp.sum(jnp.where(member, place, 0.0), axis=0, keepdims=True)
 
 
+def pack_kernel(capacity, serial_ref, cot_ref, own_ref, buf_ref, slot_ref, own_t_ref):
+    length, _ = cot_ref.shape
+    slots = buf_ref.shape[0]
+    slot = slots_of(serial_ref[...], capacity, slots // capacity)
+    slot_ref[...] = jnp.broadcast_to(slot, slot_ref.shape)
+    mask = iota((slots, length), 0) == slot.astype(jnp.int32)
+    taken = jnp.sum(jnp.where(mask, 1.0, 0.0), axis=1, keepdims=True)
+    vacant = jnp.where(taken > 0.5, 0.0, VACANT)
+    buf_ref[...] = (mm(one_hot(mask), cot_ref[...]) + vacant).astype(BF16)
+    own_t_ref[...] = turned(own_ref[...]).astype(BF16)
+
+
+def whole(*shape):
+    return pl.BlockSpec(shape, lambda i: (0,) * len(shape))
+
+
+def pack_cot(serial, cot, own, slots, capacity):
+    length, channels = cot.shape
+    return pl.pallas_call(
+        functools.partial(pack_kernel, capacity),
+        grid=(1,),
+        out_shape=(
+            jax.ShapeDtypeStruct((slots, channels), BF16),
+            jax.ShapeDtypeStruct((8, length), F32),
+            jax.ShapeDtypeStruct((channels, length), BF16),
+        ),
+        in_specs=[whole(1, length), whole(length, channels), whole(length, channels)],
+        out_specs=(whole(slots, channels), whole(8, length), whole(channels, length)),
+        compiler_params=params(12),
+        cost_estimate=cost(2 * slots * length * channels, 2 << 20),
+        name="pack_cot",
+    )(in_hbm(serial), in_hbm(cot), in_hbm(own))
+
+
 def conv_kernel(
-    capacity,
-    serial_ref,
+    nb_ref,
+    slot_ref,
     cot_ref,
-    nb_ref,
     below_ref,
+    own_t_ref,
+    above_ref,
     own_ref,
-    above_ref,
     w_ref,
     g_ref,
     buf_ref,
-    slot_ref,
     table,
+    held,
     acc,
 ):
     step = pl.program_id(0)
+    last = pl.num_programs(0) - 1
     length, channels = own_ref.shape
     slots = buf_ref.shape[0]
     rows = table.shape[1]
@@ -93,69 +128,74 @@
     ) + lax.axis_index("c")
     base = index * length - RIM
 
+    def gather():
+        for j in range(nb_ref.shape[0]):
+            linked = nb_ref[j]
+            local = jnp.where(linked < 0, -1, linked - base)
+            pick = one_hot(iota((rows, length), 0) == local)
+            gathered = mm(table[...], pick).astype(BF16)
+            g_ref[j * channels : (j + 1) * channels, :] = gathered
+            held[j * channels : (j + 1) * channels, :] = gathered
+
     @pl.when(step == 0)
     def _():
         table[:, :RIM] = turned(below_ref[...]).astype(BF16)
-        table[:, RIM : RIM + length] = turned(own_ref[...]).astype(BF16)
+        table[:, RIM : RIM + length] = own_t_ref[...]
         table[:, RIM + length :] = turned(above_ref[...]).astype(BF16)
         acc[...] = jnp.zeros_like(acc)
-
-    total = acc[...]
-    for j in range(nb_ref.shape[0]):
-        linked = nb_ref[j]
-        local = jnp.where(linked < 0, -1, linked - base)
-        pick = one_hot(iota((rows, length), 0) == local)
-        gathered = mm(table[...], pick).astype(BF16)
-        g_ref[j * channels : (j + 1) * channels, :] = gathered
-        total = total + mm_tn(w_ref[j * channels : (j + 1) * channels, :], gathered)
-    acc[...] = total
-
-    @pl.when(step == pl.num_programs(0) - 1)
+        gather()
+
+    @pl.when(jnp.logical_and(step > 0, step < last))
     def _():
-        mixed = (own_ref[...].astype(F32) + turned(acc[...])).astype(BF16)
-        slot = slots_of(serial_ref[...], capacity, slots // capacity)
-        slot_ref[...] = jnp.broadcast_to(slot, slot_ref.shape)
-        mask = iota((slots, length), 0) == slot.astype(jnp.int32)
-        taken = jnp.sum(jnp.where(mask, 1.0, 0.0), axis=1, keepdims=True)
-        vacant = jnp.where(taken > 0.5, 0.0, VACANT)
-        pick = one_hot(mask)
+        acc[...] += mm_tn(w_ref[...], held[...])
+        gather()
+
+    @pl.when(step == last)
+    def _():
+        total = acc[...] + mm_tn(w_ref[...], held[...])
+        mixed = (own_ref[...].astype(F32) + turned(total)).astype(BF16)
+        pick = one_hot(iota((slots, length), 0) == slot_ref[0:1, :].astype(jnp.int32))
         buf_ref[:, :channels] = mm(pick, mixed).astype(BF16)
-        buf_ref[:, channels:] = (mm(pick, cot_ref[...]) + vacant).astype(BF16)
-
-
-def gather_conv(serial, cot, nb, below, own, above, w_conv, slots, capacity):
+        buf_ref[:, channels:] = cot_ref[...]
+
+
+def gather_conv(nb, slot, cot_buf, below, own_t, above, own, w_conv):
     length, channels = own.shape
+    slots = cot_buf.shape[0]
     count = nb.shape[0]
     per = OFFSETS_PER_STEP
+    steps = count // per
     rows = length + 2 * RIM
-    whole = lambda *shape: pl.BlockSpec(shape, lambda i: (0,) * len(shape))
     return pl.pallas_call(
-        functools.partial(conv_kernel, capacity),
-        grid=(count // per,),
+        conv_kernel,
+        grid=(steps + 1,),
         out_shape=(
             pltpu.HBM((count * channels, length), BF16),
             jax.ShapeDtypeStruct((slots, 2 * channels), BF16),
-            jax.ShapeDtypeStruct((8, length), F32),
         ),
         in_specs=[
-            whole(1, length),
-            whole(length, channels),
-            pl.BlockSpec((per, 1, length), lambda i: (i, 0, 0)),
+            pl.BlockSpec((per, 1, length), lambda i: (jnp.minimum(i, steps - 1), 0, 0)),
+            whole(8, length),
+            whole(slots, channels),
+            whole(RIM, channels),
+            whole(channels, length),
             whole(RIM, channels),
             whole(length, channels),
-            whole(RIM, channels),
-            pl.BlockSpec((per * channels, channels), lambda i: (i, 0)),
+            pl.BlockSpec((per * channels, channels), lambda i: (jnp.maximum(i - 1, 0), 0)),
         ],
         out_specs=(
-            pl.BlockSpec((per * channels, length), lambda i: (i, 0)),
+            pl.BlockSpec((per * channels, length), lambda i: (jnp.minimum(i, steps - 1), 0)),
             whole(slots, 2 * channels),
-            whole(8, length),
         ),
-        scratch_shapes=[pltpu.VMEM((channels, rows), BF16), pltpu.VMEM((channels, length), F32)],
+        scratch_shapes=[
+            pltpu.VMEM((channels, rows), BF16),
+            pltpu.VMEM((per * channels, length), BF16),
+            pltpu.VMEM((channels, length), F32),
+        ],
         compiler_params=params(32, dimension_semantics=("arbitrary",)),
         cost_estimate=cost(2 * count * length * channels * (rows + channels), 12 << 20),
         name="gather_conv",
-    )(in_hbm(serial), in_hbm(cot), in_hbm(nb), below, in_hbm(own), above, in_hbm(w_conv))
+    )(in_hbm(nb), slot, cot_buf, below, own_t, above, in_hbm(own), in_hbm(w_conv))
 
 
 def patch_kernel(
@@ -178,7 +218,7 @@
     dk,
     dv,
 ):
-    slots, channels = out_ref.shape
+    slots, channels = dp_ref.shape
     groups, length, group = dk.shape
     depth = channels // HEADS
     factor = depth ** (-0.5)
@@ -228,10 +268,12 @@
             e = jnp.exp(scores - jnp.max(scores, axis=0, keepdims=True))
             p = e * (1.0 / jnp.sum(e, axis=0, keepdims=True))
             pb = p.astype(BF16)
-            att_t[at, :] = mm(value_t[at, :], pb)
+            attended = mm(value_t[at, :], pb)
+            att_t[at, :] = attended
             dv_g = dv_g + mm(pb, jnp.where(in_lanes, da_g, zero))
             dp = mm(v_g, jnp.where(in_rows, da_tg, zero))
-            ds = (p * (dp - jnp.sum(dp * p, axis=0, keepdims=True))).astype(BF16)
+            row_term = jnp.sum(datt_t[at, :].astype(F32) * attended, axis=0, keepdims=True)
+            ds = (p * (dp - row_term)).astype(BF16)
             dq_t[at, :] = mm(key_t[at, :], ds)
             dk_g = dk_g + mm(ds, jnp.where(in_lanes, q_g, zero))
         dk[g] = dk_g
@@ -312,21 +354,32 @@
     )(slot, buf)
 
 
+GRAD_STEPS = 9
 PIECE = 128
 PART = 16
 
 
-def grad_kernel(sizes, slot_ref, buf_ref, g_ref, gw_ref, keep_ref, send_ref, d_mixed, total):
+def grad_kernel(
+    sizes, slot_ref, buf_ref, g_ref, gw_ref, keep_ref, send_ref, d_mixed, total, near, sems
+):
     step = pl.program_id(0)
     nz, nx, nc, nrep = sizes
-    block = g_ref.shape[0]
+    block = g_ref.shape[0] // GRAD_STEPS
     channels = buf_ref.shape[1]
+
+    def fetch(i):
+        at = pl.ds(pl.multiple_of(i * block, block), block)
+        return pltpu.make_async_copy(g_ref.at[at, :], near.at[at, :], sems.at[i])
 
     @pl.when(step == 0)
     def _():
+        for i in range(GRAD_STEPS):
+            fetch(i).start()
         d_mixed[...] = unpack(slot_ref[...], buf_ref[...])
 
-    total[pl.ds(pl.multiple_of(step * block, block), block), :] = mm(g_ref[...], d_mixed[...])
+    fetch(step).wait()
+    at = pl.ds(pl.multiple_of(step * block, block), block)
+    total[at, :] = mm(near[at, :], d_mixed[...])
 
     @pl.when(step == pl.num_programs(0) - 1)
     def _():
@@ -340,7 +393,9 @@
                 @pl.when(same if is_mine else jnp.logical_not(same))
                 def _(core=core, ref=ref):
                     for z in range(nz):
-                        sz = lax.rem(z - mine[0] + nz, nz)
+                        pair = lax.rem(z % 2 + lax.rem(mine[0], 2), 2)
+                        four = lax.rem(z // 2 - lax.div(mine[0], 2) + nz // 2, nz // 2)
+                        sz = pair * (nz // 2) + four
                         for x in range(nx):
                             sx = lax.rem(x - mine[1] + nx, nx)
                             d = (z * nx + x) * nc + core
@@ -376,28 +431,28 @@
     slots, channels = buf.shape
     length = slot.shape[1]
     nz, nx, _, nrep = sizes
-    block = 3 * channels
-    whole = lambda *shape: pl.BlockSpec(shape, lambda i: (0,) * len(shape))
     shape = (2, nx * nrep, nz, PART, channels)
     return pl.pallas_call(
         functools.partial(grad_kernel, sizes),
-        grid=(g.shape[0] // block,),
+        grid=(GRAD_STEPS,),
         out_shape=(jax.ShapeDtypeStruct(shape, BF16), jax.ShapeDtypeStruct(shape, BF16)),
         in_specs=[
             whole(8, length),
             whole(slots, channels),
-            pl.BlockSpec((block, length), lambda i: (i, 0)),
+            pl.BlockSpec(memory_space=pltpu.HBM),
             whole(*gw.shape),
         ],
         out_specs=(whole(*shape), whole(*shape)),
         scratch_shapes=[
             pltpu.VMEM((length, channels), BF16),
             pltpu.VMEM((g.shape[0], channels), F32),
+            pltpu.VMEM(g.shape, BF16),
+            pltpu.SemaphoreType.DMA((GRAD_STEPS,)),
         ],
         compiler_params=params(32, dimension_semantics=("arbitrary",)),
         cost_estimate=cost(2 * g.shape[0] * length * channels, 12 << 20),
         name="grad_terms",
-    )(slot, buf, in_hbm(g), gw)
+    )(slot, buf, g, gw)
 
 
 def add_kernel(plan, *refs):
@@ -416,26 +471,27 @@
             to += 1
 
 
-def pair_kernel(sides, count, *refs):
+def pair_kernel(count, *refs):
     ins, outs = refs[: 2 * count], refs[2 * count :]
-    for part, out in enumerate(outs):
-        for side in range(sides):
+    for side in range(2):
+        for half, out in enumerate(outs):
+            parts = out.shape[0]
             value = None
             for ref in ins[side * count : (side + 1) * count]:
-                term = ref[part].astype(F32)
+                term = ref[half * parts : (half + 1) * parts].astype(F32)
                 value = term if value is None else value + term
-            rows = value.shape[0]
-            out[side * rows : (side + 1) * rows, :] = value.astype(BF16)
+            rows = value.shape[1]
+            out[:, side * rows : (side + 1) * rows, :] = value.astype(BF16)
 
 
 def add_pairs(a, b):
     parts, rows, channels = a[0].shape
-    shape = jax.ShapeDtypeStruct((2 * rows, channels), BF16)
+    shape = jax.ShapeDtypeStruct((parts // 2, 2 * rows, channels), BF16)
     return pl.pallas_call(
-        functools.partial(pair_kernel, 2, len(a)),
-        out_shape=(shape,) * parts,
+        functools.partial(pair_kernel, len(a)),
+        out_shape=(shape,) * 2,
         in_specs=[VMEM_SPEC] * (2 * len(a)),
-        out_specs=(VMEM_SPEC,) * parts,
+        out_specs=(VMEM_SPEC,) * 2,
         compiler_params=params(8),
         cost_estimate=cost(1 << 20, 1 << 20),
         name="add_pairs",
@@ -503,10 +559,9 @@
 
     below = lax.ppermute(feats[length - RIM :], SPACE, up)
     above = lax.ppermute(feats[:RIM], SPACE, down)
+    cot_buf, slot, own_t = pack_cot(serial, cotangent[0], feats, slots, capacity)
     nb = jnp.transpose(neighbours, (2, 0, 1))
-    g, row_buf, slot = gather_conv(
-        serial, cotangent[0], nb, below, feats, above, w_conv, slots, capacity
-    )
+    g, row_buf = gather_conv(nb, slot, cot_buf, below, own_t, above, feats, w_conv)
     out_buf, dp_buf, gw = patch(exchange(row_buf), w_qkv, w_proj, length)
     keep, send = grad_terms(slot, exchange(dp_buf), g, gw, sizes)
 
@@ -534,9 +589,12 @@
     def rows_of(t):
         return t.reshape(nz, PART, channels)
 
-    ab = add_pairs([rows_of(t) for t in (a[0], *a_in)], [rows_of(t) for t in (b[0], *b_in)])
-    ab_in = [shifted(ab[s], "z", s) for s in range(1, nz)]
-    (own,) = add_up([([(t, 0) for t in [ab[0], *ab_in]], 2 * PART, 1)])
+    stay, leave = add_pairs([rows_of(t) for t in (a[0], *a_in)], [rows_of(t) for t in (b[0], *b_in)])
+    came = lax.ppermute(leave, "z", [(i, i ^ 1) for i in range(nz)])
+    ab = add_up([([(stay, 0), (came, 0)], nz // 2, nz // 2)])
+    ab_in = [shifted(ab[s], "z", 2 * s) for s in range(1, nz // 2)]
+    (own,) = add_up([([(t, 0) for t in [ab[0], *ab_in]], 1, 1)])
+    own = own.reshape(2 * PART, channels)
     everyone = [own] + [shifted(own, "rep", s) for s in range(1, nrep)]
     places = slab_count
     g_conv, g_qkv, g_proj = pl.pallas_call(

time: 198 us -> 188 us (0.949)
  starting transfers between devices: 60.3 us -> 53.3 us
  Pallas kernels: 44.2 us -> 38.5 us
  waiting for transfers between devices: 27.2 us -> 30.2 us
    ppermute x22 -> x18, starting transfers between devices: 47.5 us -> 40.5 us  [shifted(): return lax.ppermute(a, axis, [(i, (i + by) % size) for i in range(size)])]
    pallas_call x3 -> x4, Pallas kernels: 25.6 us -> 21 us  [the longest x1 13.5 us: gather_conv(): pl.pallas_call(conv_kernel, grid=(steps + 1,), out_shape=(pltpu.HBM((coun...]
    ppermute x0 -> x1, waiting for transfers between devices: none -> 4.43 us  [per_device(): came = lax.ppermute(leave, 'z', [(i, i ^ 1) for i in range(nz)])]
    ppermute x22 -> x18, waiting for transfers between devices: 17.6 us -> 18.1 us  [shifted(): return lax.ppermute(a, axis, [(i, (i + by) % size) for i in range(size)])]
  transfers between devices with their start and end apart: 26 -> 23, of which waited for: 11 -> 12; matrix products, arithmetic and copies ran while one was open for 0% -> 0% of each run, Pallas kernels for 1% -> 2%
where the time goes in v1:
time: 188 us; the launch traced here: 185 us
  blocking collectives  61.3 us (33%)
  starting transfers between devices  53.3 us (28%)
  Pallas kernels  38.5 us (20%)
  waiting for transfers between devices  30.2 us (16%)
    all_to_all x2, blocking collectives, exchange(): out = lax.all_to_all(parts, SPACE, split_axis=0, concat_axis=0, tiled=True)  61.3 us
    ppermute x18, starting transfers between devices, shifted(): return lax.ppermute(a, axis, [(i, (i + by) % size) for i in range(size)])  40.5 us
    ppermute x18, waiting for transfers between devices, shifted(): return lax.ppermute(a, axis, [(i, (i + by) % size) for i in range(size)])  18.1 us
    pallas_call x1, Pallas kernels, patch(): pl.pallas_call(patch_kernel, out_shape=(jax.ShapeDtypeStruct((slots, chan...  14.6 us
    pallas_call x1, Pallas kernels, gather_conv(): pl.pallas_call(conv_kernel, grid=(steps + 1,), out_shape=(pltpu.HBM((coun...  13.5 us
    all_to_all x1, starting transfers between devices, exchange(): out = lax.all_to_all(parts, SPACE, split_axis=0, concat_axis=0, tiled=True)  6.62 us
    pallas_call x1, Pallas kernels, grad_terms(): pl.pallas_call(functools.partial(grad_kernel, sizes), grid=(GRAD_STEPS,),...  5.63 us
    ppermute x1, waiting for transfers between devices, per_device(): came = lax.ppermute(leave, 'z', [(i, i ^ 1) for i in range(nz)])  4.43 us
  transfers between devices with their start and end apart: 23, of which 12 were waited for; matrix products, arithmetic and copies ran while one was open for 0% of the time, Pallas kernels for 2%

profile of v1, /device:TPU:32, one launch (start us, length us, event | category | flops | bytes accessed | tf_op | source)
XLA Modules:
  0.0 185.1 jit_solution(15478750468324198265)
XLA Ops:
  0.6 0.9 slice_bitcast_fusion
  1.5 3.7 %collective-permute-start.1 = (bf16[128,256]{1,0:T(8,128)(2,1)S(1)}, bf16[128,256]{1,0:T(8,128)(2,1)S(1)}, u32[]{:S(2)}, u32[]{:S(2)}) collective-permute-start(bf16[128,256]{1,0:T(8,128)(2,1)S(1)} %get-tuple-element.92), channel_id=1, source_target_pairs={{4,0},{8,4},{12,8},{16,12},{20,16},{24,20},{28,24},{32,28},{36,32}... | collective-permute-start | bytes 196616 | tf_op jit(solution)/shard_map/ppermute | solution.py:561
  5.2 1.9 %collective-permute-start = (bf16[128,256]{1,0:T(8,128)(2,1)S(1)}, bf16[128,256]{1,0:T(8,128)(2,1)S(1)}, u32[]{:S(2)}, u32[]{:S(2)}) collective-permute-start(bf16[128,256]{1,0:T(8,128)(2,1)S(1)} %get-tuple-element.93), channel_id=1, source_target_pairs={{0,4},{4,8},{8,12},{12,16},{16,20},{20,24},{24,28},{28,32},{32,36}... | collective-permute-start | bytes 196616 | tf_op jit(solution)/shard_map/ppermute | solution.py:560
  7.1 1.8 pack_cot.1
  9.0 0.0 collective-permute-done.1.above_ref
  9.0 3.9 %collective-permute-done.below_ref = bf16[128,256]{1,0:T(8,128)(2,1)S(1)} collective-permute-done((bf16[128,256]{1,0:T(8,128)(2,1)S(1)}, bf16[128,256]{1,0:T(8,128)(2,1)S(1)}, u32[]{:S(2)}, u32[]{:S(2)}) %collective-permute-start) | collective-permute-done | bytes 65568 | tf_op jit(solution)/shard_map/ppermute | solution.py:560
  12.9 13.5 %gather_conv.1 = (bf16[6912,512]{1,0:T(8,128)(2,1)}, bf16[1024,512]{1,0:T(8,128)(2,1)S(1)}) custom-call(s32[27,1,512]{2,1,0:T(1,128)} %bitcast.51, f32[8,512]{1,0:T(8,128)S(1)} %get-tuple-element.48.slot_ref, bf16[1024,256]{1,0:T(8,128)(2,1)S(1)} %get-tuple-element.49.cot_ref, bf16[128,256]{1,0:T(8,128)(2,1)S(1)} %collective-permute-done.below_ref, ...), custom_call_target="tpu_custom_call" | custom-call | flops 7247757312 | bytes 12582912 | tf_op jit(solution)/shard_map/gather_conv/pallas_call | solution.py:169
  26.4 0.0 copy-start
  26.4 0.0 copy-start.1
  26.4 38.2 %all_to_all.15 = bf16[64,16,512]{2,1,0:T(8,128)(2,1)S(1)} all-to-all(bf16[64,16,512]{2,1,0:T(8,128)(2,1)S(1)} %bitcast.32), channel_id=1, replica_groups=mesh['z'=8,'x'=4,'c'=2,'rep'=4] {'z','x','c'}, dimensions={0} | all-to-all | bytes 2097152 | tf_op jit(solution)/shard_map/all_to_all | solution.py:557
  64.5 0.0 copy-done
  64.6 0.0 copy-done.1
  64.6 14.6 %patch.1 = (bf16[1024,256]{1,0:T(8,128)(2,1)}, bf16[1024,256]{1,0:T(8,128)(2,1)S(1)}, f32[256,1024]{1,0:T(8,128)S(1)}) custom-call(bf16[1024,512]{1,0:T(8,128)(2,1)S(1)} %bitcast.33, bf16[256,768]{1,0:T(8,128)(2,1)S(1)} %copy-done, bf16[256,256]{1,0:T(8,128)(2,1)S(1)} %copy-done.1), custom_call_target="tpu_custom_call" | custom-call | flops 14000000000 | bytes 4194304 | tf_op jit(solution)/shard_map/patch/pallas_call | solution.py:313
  79.2 23.2 %all_to_all.16 = bf16[64,16,256]{2,1,0:T(8,128)(2,1)S(1)} all-to-all(bf16[64,16,256]{2,1,0:T(8,128)(2,1)S(1)} %bitcast.35), channel_id=1, replica_groups=mesh['z'=8,'x'=4,'c'=2,'rep'=4] {'z','x','c'}, dimensions={0} | all-to-all | bytes 1048576 | tf_op jit(solution)/shard_map/all_to_all | solution.py:557
  102.4 0.0 slice-done
  102.4 0.0 slice-done.1
  102.4 5.6 %grad_terms.1 = (bf16[2,16,8,16,256]{4,3,2,1,0:T(8,128)(2,1)S(1)}, bf16[2,16,8,16,256]{4,3,2,1,0:T(8,128)(2,1)S(1)}) custom-call(f32[8,512]{1,0:T(8,128)S(1)} %get-tuple-element.48.slot_ref, bf16[1024,256]{1,0:T(8,128)(2,1)S(1)} %bitcast.31, bf16[6912,512]{1,0:T(8,128)(2,1)S(1)} %bitcast.30, f32[256,1024]{1,0:T(8,128)S(1)} %get-tuple-element.54.gw_ref), custom_call_target="tpu_custom_call" | custom-call | flops 1811939328 | bytes 12582912 | tf_op jit(solution)/shard_map/grad_terms/pallas_call | solution.py:435
  108.0 0.6 collective-permute-start.2
  108.6 3.8 %collective-permute-done.2 = bf16[2,16,8,16,256]{4,3,2,1,0:T(8,128)(2,1)S(1)} collective-permute-done((bf16[2,16,8,16,256]{4,3,2,1,0:T(8,128)(2,1)S(1)}, bf16[2,16,8,16,256]{4,3,2,1,0:T(8,128)(2,1)S(1)}, u32[]{:S(2)}, u32[]{:S(2)}) %collective-permute-start.2) | collective-permute-done | bytes 2097184 | tf_op jit(solution)/shard_map/ppermute | solution.py:568
  112.4 0.5 add_up.4
  112.8 6.6 %all-to-all-start.2 = ((bf16[64,16,256]{2,1,0:T(8,128)(2,1)}), bf16[64,16,256]{2,1,0:T(8,128)(2,1)S(1)}, u32[]{:S(2)}, u32[]{:S(2)}) async-start(bf16[64,16,256]{2,1,0:T(8,128)(2,1)} %bitcast.11), calls=%async_computation.2 | async-start | bytes 1048576 | tf_op jit(solution)/shard_map/all_to_all | solution.py:557
  119.5 1.5 collective-permute-start.3
  121.0 2.7 %collective-permute-start.4 = (bf16[4,8,16,256]{3,2,1,0:T(8,128)(2,1)S(1)}, bf16[4,8,16,256]{3,2,1,0:T(8,128)(2,1)S(1)}, u32[]{:S(2)}, u32[]{:S(2)}) collective-permute-start(bf16[4,8,16,256]{3,2,1,0:T(8,128)(2,1)S(1)} %get-tuple-element.69), channel_id=1, source_target_pairs={{0,16},{8,24},{16,0},{24,8},{1,17},{9,25},{17,1},{25,9},{2,18},{10... | collective-permute-start | bytes 786440 | tf_op jit(solution)/shard_map/ppermute | solution.py:541
  123.7 1.5 collective-permute-start.5
  125.1 1.6 collective-permute-start.6
  126.7 2.9 %collective-permute-start.7 = (bf16[4,8,16,256]{3,2,1,0:T(8,128)(2,1)S(1)}, bf16[4,8,16,256]{3,2,1,0:T(8,128)(2,1)S(1)}, u32[]{:S(2)}, u32[]{:S(2)}) collective-permute-start(bf16[4,8,16,256]{3,2,1,0:T(8,128)(2,1)S(1)} %get-tuple-element.73), channel_id=1, source_target_pairs={{0,2},{1,3},{2,0},{3,1},{4,6},{5,7},{6,4},{7,5},{8,10},{9,11},{10,... | collective-permute-start | bytes 786440 | tf_op jit(solution)/shard_map/ppermute | solution.py:541
  129.6 5.0 %collective-permute-done.3.refs_1_ = bf16[4,8,16,256]{3,2,1,0:T(8,128)(2,1)S(1)} collective-permute-done((bf16[4,8,16,256]{3,2,1,0:T(8,128)(2,1)S(1)}, bf16[4,8,16,256]{3,2,1,0:T(8,128)(2,1)S(1)}, u32[]{:S(2)}, u32[]{:S(2)}) %collective-permute-start.3) | collective-permute-done | bytes 262176 | tf_op jit(solution)/shard_map/ppermute | solution.py:541
  134.6 3.0 %collective-permute-start.8 = (bf16[4,8,16,256]{3,2,1,0:T(8,128)(2,1)S(1)}, bf16[4,8,16,256]{3,2,1,0:T(8,128)(2,1)S(1)}, u32[]{:S(2)}, u32[]{:S(2)}) collective-permute-start(bf16[4,8,16,256]{3,2,1,0:T(8,128)(2,1)S(1)} %get-tuple-element.74), channel_id=1, source_target_pairs={{0,3},{1,0},{2,1},{3,2},{4,7},{5,4},{6,5},{7,6},{8,11},{9,8},{10,9... | collective-permute-start | bytes 786440 | tf_op jit(solution)/shard_map/ppermute | solution.py:541
  137.6 2.6 %collective-permute-done.4.refs_2_ = bf16[4,8,16,256]{3,2,1,0:T(8,128)(2,1)S(1)} collective-permute-done((bf16[4,8,16,256]{3,2,1,0:T(8,128)(2,1)S(1)}, bf16[4,8,16,256]{3,2,1,0:T(8,128)(2,1)S(1)}, u32[]{:S(2)}, u32[]{:S(2)}) %collective-permute-start.4) | collective-permute-done | bytes 262176 | tf_op jit(solution)/shard_map/ppermute | solution.py:541
  140.3 0.0 collective-permute-done.5.refs_3_
  140.3 0.0 collective-permute-done.6.refs_5_
  140.3 0.4 collective-permute-done.7.refs_6_
  140.7 1.3 collective-permute-done.8.refs_7_
  142.0 0.3 add_up.5
  142.2 1.2 collective-permute-start.9
  143.4 4.1 %collective-permute-start.10 = (bf16[1,8,16,256]{3,2,1,0:T(8,128)(2,1)S(1)}, bf16[1,8,16,256]{3,2,1,0:T(8,128)(2,1)S(1)}, u32[]{:S(2)}, u32[]{:S(2)}) collective-permute-start(bf16[1,8,16,256]{3,2,1,0:T(8,128)(2,1)S(1)} %get-tuple-element.77), channel_id=1, source_target_pairs={{0,2},{1,3},{2,0},{3,1},{4,6},{5,7},{6,4},{7,5},{8,10},{9,11},{10,... | collective-permute-start | bytes 196616 | tf_op jit(solution)/shard_map/ppermute | solution.py:541
  147.5 0.1 collective-permute-start.11
  147.6 0.2 collective-permute-start.12
  147.8 6.7 %collective-permute-start.13 = (bf16[1,8,16,256]{3,2,1,0:T(8,128)(2,1)S(1)}, bf16[1,8,16,256]{3,2,1,0:T(8,128)(2,1)S(1)}, u32[]{:S(2)}, u32[]{:S(2)}) collective-permute-start(bf16[1,8,16,256]{3,2,1,0:T(8,128)(2,1)S(1)} %get-tuple-element.81), channel_id=1, source_target_pairs={{0,16},{8,24},{16,0},{24,8},{1,17},{9,25},{17,1},{25,9},{2,18},{10... | collective-permute-start | bytes 196616 | tf_op jit(solution)/shard_map/ppermute | solution.py:541
  154.6 0.0 collective-permute-done.9
  154.6 2.6 %collective-permute-start.14 = (bf16[1,8,16,256]{3,2,1,0:T(8,128)(2,1)S(1)}, bf16[1,8,16,256]{3,2,1,0:T(8,128)(2,1)S(1)}, u32[]{:S(2)}, u32[]{:S(2)}) collective-permute-start(bf16[1,8,16,256]{3,2,1,0:T(8,128)(2,1)S(1)} %get-tuple-element.82), channel_id=1, source_target_pairs={{0,24},{8,0},{16,8},{24,16},{1,25},{9,1},{17,9},{25,17},{2,26},{10... | collective-permute-start | bytes 196616 | tf_op jit(solution)/shard_map/ppermute | solution.py:541
  157.2 0.0 collective-permute-done.10
  157.2 0.0 collective-permute-done.11
  157.2 0.0 collective-permute-done.12
  157.2 0.3 collective-permute-done.13
  157.5 1.6 collective-permute-done.14
  159.1 0.1 add_pairs.1
  159.2 0.1 collective-permute-start.15
  159.3 4.4 %collective-permute-done.15.refs_1_ = bf16[4,32,256]{2,1,0:T(8,128)(2,1)S(1)} collective-permute-done((bf16[4,32,256]{2,1,0:T(8,128)(2,1)S(1)}, bf16[4,32,256]{2,1,0:T(8,128)(2,1)S(1)}, u32[]{:S(2)}, u32[]{:S(2)}) %collective-permute-start.15) | collective-permute-done | bytes 65568 | tf_op jit(solution)/shard_map/ppermute | solution.py:593
  163.7 0.1 collective-permute-start.16
  163.8 5.2 %collective-permute-start.17 = (bf16[1,32,256]{2,1,0:T(8,128)(2,1)S(1)}, bf16[1,32,256]{2,1,0:T(8,128)(2,1)S(1)}, u32[]{:S(2)}, u32[]{:S(2)}) collective-permute-start(bf16[1,32,256]{2,1,0:T(8,128)(2,1)S(1)} %get-tuple-element.87), channel_id=1, source_target_pairs={{0,128},{32,160},{64,192},{96,224},{128,0},{160,32},{192,64},{224,... | collective-permute-start | bytes 49160 | tf_op jit(solution)/shard_map/ppermute | solution.py:541
  169.0 2.8 %collective-permute-start.18 = (bf16[1,32,256]{2,1,0:T(8,128)(2,1)S(1)}, bf16[1,32,256]{2,1,0:T(8,128)(2,1)S(1)}, u32[]{:S(2)}, u32[]{:S(2)}) collective-permute-start(bf16[1,32,256]{2,1,0:T(8,128)(2,1)S(1)} %get-tuple-element.88), channel_id=1, source_target_pairs={{0,192},{32,224},{64,0},{96,32},{128,64},{160,96},{192,128},{224,1... | collective-permute-start | bytes 49160 | tf_op jit(solution)/shard_map/ppermute | solution.py:541
  171.8 0.0 collective-permute-done.16.refs_1_
  171.8 0.0 collective-permute-done.17.refs_2_
  171.8 1.8 collective-permute-done.18.refs_3_
  173.7 0.6 collective-permute-start.21
  174.3 3.7 %collective-permute-start.20 = (bf16[32,256]{1,0:T(8,128)(2,1)S(1)}, bf16[32,256]{1,0:T(8,128)(2,1)S(1)}, u32[]{:S(2)}, u32[]{:S(2)}) collective-permute-start(bf16[32,256]{1,0:T(8,128)(2,1)S(1)} %bitcast.37), channel_id=1, source_target_pairs={{0,2},{1,3},{2,0},{3,1},{4,6},{5,7},{6,4},{7,5},{8,10},{9,11},{10,... | collective-permute-start | bytes 49160 | tf_op jit(solution)/shard_map/ppermute | solution.py:541
  178.0 0.0 collective-permute-start.19
  178.0 0.0 collective-permute-done.21.refs_3_
  178.0 1.7 collective-permute-done.20.refs_2_
  179.7 3.2 %collective-permute-done.19.refs_1_ = bf16[32,256]{1,0:T(8,128)(2,1)S(1)} collective-permute-done((bf16[32,256]{1,0:T(8,128)(2,1)S(1)}, bf16[32,256]{1,0:T(8,128)(2,1)S(1)}, u32[]{:S(2)}, u32[]{:S(2)}) %collective-permute-start.19) | collective-permute-done | bytes 16416 | tf_op jit(solution)/shard_map/ppermute | solution.py:541
  183.0 0.7 final.1
  183.6 0.0 all-to-all-done.2
  183.6 1.4 return_rows.1
  (5 shorter events, 0.0 us)
Async XLA Ops:
  1.5 7.4 %collective-permute-start.1 = (bf16[128,256]{1,0:T(8,128)(2,1)S(1)}, bf16[128,256]{1,0:T(8,128)(2,1)S(1)}, u32[]{:S(2)}, u32[]{:S(2)}) collective-permute-start(bf16[128,256]{1,0:T(8,128)(2,1)S(1)} %get-tuple-element.92), channel_id=1, source_target_pairs={{4,0},{8,4},{12,8},{16,12},{20,16},{24,20},{28,24},{32,28},{36,32}... | collective-permute-start | bytes 196616 | tf_op jit(solution)/shard_map/ppermute | solution.py:561
  5.2 7.7 %collective-permute-start = (bf16[128,256]{1,0:T(8,128)(2,1)S(1)}, bf16[128,256]{1,0:T(8,128)(2,1)S(1)}, u32[]{:S(2)}, u32[]{:S(2)}) collective-permute-start(bf16[128,256]{1,0:T(8,128)(2,1)S(1)} %get-tuple-element.93), channel_id=1, source_target_pairs={{0,4},{4,8},{8,12},{12,16},{16,20},{20,24},{24,28},{28,32},{32,36}... | collective-permute-start | bytes 196616 | tf_op jit(solution)/shard_map/ppermute | solution.py:560
  26.4 38.2 %copy-start = (bf16[256,768]{1,0:T(8,128)(2,1)S(1)}, bf16[256,768]{1,0:T(8,128)(2,1)}, u32[]{:S(2)}) copy-start(bf16[256,768]{1,0:T(8,128)(2,1)} %wqkv_ref.1) | copy-start | bytes 1179652
  26.4 38.2 %copy-start.1 = (bf16[256,256]{1,0:T(8,128)(2,1)S(1)}, bf16[256,256]{1,0:T(8,128)(2,1)}, u32[]{:S(2)}) copy-start(bf16[256,256]{1,0:T(8,128)(2,1)} %wproj_ref.1) | copy-start | bytes 393220
  64.5 37.8 %slice-start = ((s8[7077888]{0:T(1024)(128)(4,1)}), s8[4194304]{0:T(1024)(128)(4,1)S(1)}, s32[]{:S(2)}) async-start(s8[7077888]{0:T(1024)(128)(4,1)} %bitcast.29), calls=%async_computation.3 | async-start | bytes 8388608
  64.6 37.8 %slice-start.1 = ((s8[7077888]{0:T(1024)(128)(4,1)}), s8[2883584]{0:T(1024)(128)(4,1)S(1)}, s32[]{:S(2)}) async-start(s8[7077888]{0:T(1024)(128)(4,1)} %bitcast.29), calls=%async_computation.4 | async-start | bytes 5767168
  108.0 4.4 %collective-permute-start.2 = (bf16[2,16,8,16,256]{4,3,2,1,0:T(8,128)(2,1)S(1)}, bf16[2,16,8,16,256]{4,3,2,1,0:T(8,128)(2,1)S(1)}, u32[]{:S(2)}, u32[]{:S(2)}) collective-permute-start(bf16[2,16,8,16,256]{4,3,2,1,0:T(8,128)(2,1)S(1)} %get-tuple-element.56), channel_id=1, source_target_pairs={{0,4},{4,0},{1,5},{5,1},{2,6},{6,2},{3,7},{7,3},{8,12},{12,8},{9,1... | collective-permute-start | bytes 6291464 | tf_op jit(solution)/shard_map/ppermute | solution.py:568
  112.8 70.8 %all-to-all-start.2 = ((bf16[64,16,256]{2,1,0:T(8,128)(2,1)}), bf16[64,16,256]{2,1,0:T(8,128)(2,1)S(1)}, u32[]{:S(2)}, u32[]{:S(2)}) async-start(bf16[64,16,256]{2,1,0:T(8,128)(2,1)} %bitcast.11), calls=%async_computation.2 | async-start | bytes 1048576 | tf_op jit(solution)/shard_map/all_to_all | solution.py:557
  119.5 15.2 %collective-permute-start.3 = (bf16[4,8,16,256]{3,2,1,0:T(8,128)(2,1)S(1)}, bf16[4,8,16,256]{3,2,1,0:T(8,128)(2,1)S(1)}, u32[]{:S(2)}, u32[]{:S(2)}) collective-permute-start(bf16[4,8,16,256]{3,2,1,0:T(8,128)(2,1)S(1)} %get-tuple-element.68), channel_id=1, source_target_pairs={{0,8},{8,16},{16,24},{24,0},{1,9},{9,17},{17,25},{25,1},{2,10},{10... | collective-permute-start | bytes 786440 | tf_op jit(solution)/shard_map/ppermute | solution.py:541
  121.0 19.3 %collective-permute-start.4 = (bf16[4,8,16,256]{3,2,1,0:T(8,128)(2,1)S(1)}, bf16[4,8,16,256]{3,2,1,0:T(8,128)(2,1)S(1)}, u32[]{:S(2)}, u32[]{:S(2)}) collective-permute-start(bf16[4,8,16,256]{3,2,1,0:T(8,128)(2,1)S(1)} %get-tuple-element.69), channel_id=1, source_target_pairs={{0,16},{8,24},{16,0},{24,8},{1,17},{9,25},{17,1},{25,9},{2,18},{10... | collective-permute-start | bytes 786440 | tf_op jit(solution)/shard_map/ppermute | solution.py:541
  123.7 16.6 %collective-permute-start.5 = (bf16[4,8,16,256]{3,2,1,0:T(8,128)(2,1)S(1)}, bf16[4,8,16,256]{3,2,1,0:T(8,128)(2,1)S(1)}, u32[]{:S(2)}, u32[]{:S(2)}) collective-permute-start(bf16[4,8,16,256]{3,2,1,0:T(8,128)(2,1)S(1)} %get-tuple-element.70), channel_id=1, source_target_pairs={{0,24},{8,0},{16,8},{24,16},{1,25},{9,1},{17,9},{25,17},{2,26},{10... | collective-permute-start | bytes 786440 | tf_op jit(solution)/shard_map/ppermute | solution.py:541
  125.1 15.1 %collective-permute-start.6 = (bf16[4,8,16,256]{3,2,1,0:T(8,128)(2,1)S(1)}, bf16[4,8,16,256]{3,2,1,0:T(8,128)(2,1)S(1)}, u32[]{:S(2)}, u32[]{:S(2)}) collective-permute-start(bf16[4,8,16,256]{3,2,1,0:T(8,128)(2,1)S(1)} %get-tuple-element.72), channel_id=1, source_target_pairs={{0,1},{1,2},{2,3},{3,0},{4,5},{5,6},{6,7},{7,4},{8,9},{9,10},{10,1... | collective-permute-start | bytes 786440 | tf_op jit(solution)/shard_map/ppermute | solution.py:541
  126.7 13.9 %collective-permute-start.7 = (bf16[4,8,16,256]{3,2,1,0:T(8,128)(2,1)S(1)}, bf16[4,8,16,256]{3,2,1,0:T(8,128)(2,1)S(1)}, u32[]{:S(2)}, u32[]{:S(2)}) collective-permute-start(bf16[4,8,16,256]{3,2,1,0:T(8,128)(2,1)S(1)} %get-tuple-element.73), channel_id=1, source_target_pairs={{0,2},{1,3},{2,0},{3,1},{4,6},{5,7},{6,4},{7,5},{8,10},{9,11},{10,... | collective-permute-start | bytes 786440 | tf_op jit(solution)/shard_map/ppermute | solution.py:541
  134.6 7.3 %collective-permute-start.8 = (bf16[4,8,16,256]{3,2,1,0:T(8,128)(2,1)S(1)}, bf16[4,8,16,256]{3,2,1,0:T(8,128)(2,1)S(1)}, u32[]{:S(2)}, u32[]{:S(2)}) collective-permute-start(bf16[4,8,16,256]{3,2,1,0:T(8,128)(2,1)S(1)} %get-tuple-element.74), channel_id=1, source_target_pairs={{0,3},{1,0},{2,1},{3,2},{4,7},{5,4},{6,5},{7,6},{8,11},{9,8},{10,9... | collective-permute-start | bytes 786440 | tf_op jit(solution)/shard_map/ppermute | solution.py:541
  142.2 12.3 %collective-permute-start.9 = (bf16[1,8,16,256]{3,2,1,0:T(8,128)(2,1)S(1)}, bf16[1,8,16,256]{3,2,1,0:T(8,128)(2,1)S(1)}, u32[]{:S(2)}, u32[]{:S(2)}) collective-permute-start(bf16[1,8,16,256]{3,2,1,0:T(8,128)(2,1)S(1)} %get-tuple-element.76), channel_id=1, source_target_pairs={{0,1},{1,2},{2,3},{3,0},{4,5},{5,6},{6,7},{7,4},{8,9},{9,10},{10,1... | collective-permute-start | bytes 196616 | tf_op jit(solution)/shard_map/ppermute | solution.py:541
  143.4 13.8 %collective-permute-start.10 = (bf16[1,8,16,256]{3,2,1,0:T(8,128)(2,1)S(1)}, bf16[1,8,16,256]{3,2,1,0:T(8,128)(2,1)S(1)}, u32[]{:S(2)}, u32[]{:S(2)}) collective-permute-start(bf16[1,8,16,256]{3,2,1,0:T(8,128)(2,1)S(1)} %get-tuple-element.77), channel_id=1, source_target_pairs={{0,2},{1,3},{2,0},{3,1},{4,6},{5,7},{6,4},{7,5},{8,10},{9,11},{10,... | collective-permute-start | bytes 196616 | tf_op jit(solution)/shard_map/ppermute | solution.py:541
  147.5 9.7 %collective-permute-start.11 = (bf16[1,8,16,256]{3,2,1,0:T(8,128)(2,1)S(1)}, bf16[1,8,16,256]{3,2,1,0:T(8,128)(2,1)S(1)}, u32[]{:S(2)}, u32[]{:S(2)}) collective-permute-start(bf16[1,8,16,256]{3,2,1,0:T(8,128)(2,1)S(1)} %get-tuple-element.78), channel_id=1, source_target_pairs={{0,3},{1,0},{2,1},{3,2},{4,7},{5,4},{6,5},{7,6},{8,11},{9,8},{10,9... | collective-permute-start | bytes 196616 | tf_op jit(solution)/shard_map/ppermute | solution.py:541
  147.6 9.6 %collective-permute-start.12 = (bf16[1,8,16,256]{3,2,1,0:T(8,128)(2,1)S(1)}, bf16[1,8,16,256]{3,2,1,0:T(8,128)(2,1)S(1)}, u32[]{:S(2)}, u32[]{:S(2)}) collective-permute-start(bf16[1,8,16,256]{3,2,1,0:T(8,128)(2,1)S(1)} %get-tuple-element.80), channel_id=1, source_target_pairs={{0,8},{8,16},{16,24},{24,0},{1,9},{9,17},{17,25},{25,1},{2,10},{10... | collective-permute-start | bytes 196616 | tf_op jit(solution)/shard_map/ppermute | solution.py:541
  147.8 9.7 %collective-permute-start.13 = (bf16[1,8,16,256]{3,2,1,0:T(8,128)(2,1)S(1)}, bf16[1,8,16,256]{3,2,1,0:T(8,128)(2,1)S(1)}, u32[]{:S(2)}, u32[]{:S(2)}) collective-permute-start(bf16[1,8,16,256]{3,2,1,0:T(8,128)(2,1)S(1)} %get-tuple-element.81), channel_id=1, source_target_pairs={{0,16},{8,24},{16,0},{24,8},{1,17},{9,25},{17,1},{25,9},{2,18},{10... | collective-permute-start | bytes 196616 | tf_op jit(solution)/shard_map/ppermute | solution.py:541
  154.6 4.5 %collective-permute-start.14 = (bf16[1,8,16,256]{3,2,1,0:T(8,128)(2,1)S(1)}, bf16[1,8,16,256]{3,2,1,0:T(8,128)(2,1)S(1)}, u32[]{:S(2)}, u32[]{:S(2)}) collective-permute-start(bf16[1,8,16,256]{3,2,1,0:T(8,128)(2,1)S(1)} %get-tuple-element.82), channel_id=1, source_target_pairs={{0,24},{8,0},{16,8},{24,16},{1,25},{9,1},{17,9},{25,17},{2,26},{10... | collective-permute-start | bytes 196616 | tf_op jit(solution)/shard_map/ppermute | solution.py:541
  159.2 4.5 %collective-permute-start.15 = (bf16[4,32,256]{2,1,0:T(8,128)(2,1)S(1)}, bf16[4,32,256]{2,1,0:T(8,128)(2,1)S(1)}, u32[]{:S(2)}, u32[]{:S(2)}) collective-permute-start(bf16[4,32,256]{2,1,0:T(8,128)(2,1)S(1)} %get-tuple-element.84), channel_id=1, source_target_pairs={{0,32},{32,0},{64,96},{96,64},{128,160},{160,128},{192,224},{224,1... | collective-permute-start | bytes 196616 | tf_op jit(solution)/shard_map/ppermute | solution.py:593
  163.7 8.1 %collective-permute-start.16 = (bf16[1,32,256]{2,1,0:T(8,128)(2,1)S(1)}, bf16[1,32,256]{2,1,0:T(8,128)(2,1)S(1)}, u32[]{:S(2)}, u32[]{:S(2)}) collective-permute-start(bf16[1,32,256]{2,1,0:T(8,128)(2,1)S(1)} %get-tuple-element.86), channel_id=1, source_target_pairs={{0,64},{32,96},{64,128},{96,160},{128,192},{160,224},{192,0},{224,... | collective-permute-start | bytes 49160 | tf_op jit(solution)/shard_map/ppermute | solution.py:541
  163.8 8.0 %collective-permute-start.17 = (bf16[1,32,256]{2,1,0:T(8,128)(2,1)S(1)}, bf16[1,32,256]{2,1,0:T(8,128)(2,1)S(1)}, u32[]{:S(2)}, u32[]{:S(2)}) collective-permute-start(bf16[1,32,256]{2,1,0:T(8,128)(2,1)S(1)} %get-tuple-element.87), channel_id=1, source_target_pairs={{0,128},{32,160},{64,192},{96,224},{128,0},{160,32},{192,64},{224,... | collective-permute-start | bytes 49160 | tf_op jit(solution)/shard_map/ppermute | solution.py:541
  169.0 4.6 %collective-permute-start.18 = (bf16[1,32,256]{2,1,0:T(8,128)(2,1)S(1)}, bf16[1,32,256]{2,1,0:T(8,128)(2,1)S(1)}, u32[]{:S(2)}, u32[]{:S(2)}) collective-permute-start(bf16[1,32,256]{2,1,0:T(8,128)(2,1)S(1)} %get-tuple-element.88), channel_id=1, source_target_pairs={{0,192},{32,224},{64,0},{96,32},{128,64},{160,96},{192,128},{224,1... | collective-permute-start | bytes 49160 | tf_op jit(solution)/shard_map/ppermute | solution.py:541
  173.7 4.3 %collective-permute-start.21 = (bf16[32,256]{1,0:T(8,128)(2,1)S(1)}, bf16[32,256]{1,0:T(8,128)(2,1)S(1)}, u32[]{:S(2)}, u32[]{:S(2)}) collective-permute-start(bf16[32,256]{1,0:T(8,128)(2,1)S(1)} %bitcast.36), channel_id=1, source_target_pairs={{0,3},{1,0},{2,1},{3,2},{4,7},{5,4},{6,5},{7,6},{8,11},{9,8},{10,9... | collective-permute-start | bytes 49160 | tf_op jit(solution)/shard_map/ppermute | solution.py:541
  174.3 5.4 %collective-permute-start.20 = (bf16[32,256]{1,0:T(8,128)(2,1)S(1)}, bf16[32,256]{1,0:T(8,128)(2,1)S(1)}, u32[]{:S(2)}, u32[]{:S(2)}) collective-permute-start(bf16[32,256]{1,0:T(8,128)(2,1)S(1)} %bitcast.37), channel_id=1, source_target_pairs={{0,2},{1,3},{2,0},{3,1},{4,6},{5,7},{6,4},{7,5},{8,10},{9,11},{10,... | collective-permute-start | bytes 49160 | tf_op jit(solution)/shard_map/ppermute | solution.py:541
  178.0 4.9 %collective-permute-start.19 = (bf16[32,256]{1,0:T(8,128)(2,1)S(1)}, bf16[32,256]{1,0:T(8,128)(2,1)S(1)}, u32[]{:S(2)}, u32[]{:S(2)}) collective-permute-start(bf16[32,256]{1,0:T(8,128)(2,1)S(1)} %bitcast.38), channel_id=1, source_target_pairs={{0,1},{1,2},{2,3},{3,0},{4,5},{5,6},{6,7},{7,4},{8,9},{9,10},{10,1... | collective-permute-start | bytes 49160 | tf_op jit(solution)/shard_map/ppermute | solution.py:541

commit v2 on v1

--- a/solution.py
+++ b/solution.py
@@ -199,6 +199,7 @@
 
 
 def patch_kernel(
+    capacity,
     buf_ref,
     wqkv_ref,
     wproj_ref,
@@ -225,8 +226,14 @@
 
     mark = buf_ref[:, channels : channels + 128][:, 0:1]
     valid = jnp.broadcast_to(mark.astype(F32), (slots, 128)) < VACANT / 2
-    lower = one_hot(iota((slots, slots), 1) < iota((slots, slots), 0))
-    col = jnp.where(valid, mm(lower, one_hot(valid)), -1.0)
+    senders = slots // capacity
+    lowest = capacity * iota((senders, slots), 0)
+    place = iota((senders, slots), 1)
+    own = one_hot(jnp.logical_and(place >= lowest, place < lowest + capacity))
+    counts = mm(own, one_hot(valid)).astype(BF16)
+    earlier = one_hot(capacity * iota((slots, senders), 1) + capacity <= iota((slots, senders), 0))
+    within = jnp.bitwise_and(iota((slots, 128), 0), capacity - 1).astype(F32)
+    col = jnp.where(valid, mm(earlier, counts) + within, -1.0)
     row = jnp.transpose(col, (1, 0))[0:1, :].astype(jnp.int32)
     rows = mm(one_hot(iota((length, slots), 0) == row), buf_ref[...])
     patched, upstream = rows[:, :channels], rows[:, channels:].astype(BF16)
@@ -251,8 +258,15 @@
         datt_s[g] = d_att[:, g * group : (g + 1) * group]
 
     lane = iota((length, group), 1)
-    sub = iota((group, length), 0)
     zero = jnp.zeros((), BF16)
+
+    def rows_only(a, h):
+        parts = [a[h * depth : (h + 1) * depth]]
+        if h > 0:
+            parts = [jnp.zeros((h * depth, length), BF16), *parts]
+        if (h + 1) * depth < group:
+            parts = [*parts, jnp.zeros((group - (h + 1) * depth, length), BF16)]
+        return jnp.concatenate(parts, axis=0)
 
     def heads_of(g, carry):
         start = pl.multiple_of(g * group, group)
@@ -261,17 +275,16 @@
         dk_g = jnp.zeros((length, group), F32)
         dv_g = jnp.zeros((length, group), F32)
         for h in range(group // depth):
-            in_rows = lax.div(sub, jnp.int32(depth)) == h
-            in_lanes = lax.div(lane, jnp.int32(depth)) == h
+            in_lanes = jnp.logical_and(lane >= h * depth, lane < (h + 1) * depth)
             at = pl.ds(pl.multiple_of(start + h * depth, depth), depth)
-            scores = mm(k_g, jnp.where(in_rows, q_tg, zero))
+            scores = mm(k_g, rows_only(q_tg, h))
             e = jnp.exp(scores - jnp.max(scores, axis=0, keepdims=True))
             p = e * (1.0 / jnp.sum(e, axis=0, keepdims=True))
             pb = p.astype(BF16)
             attended = mm(value_t[at, :], pb)
             att_t[at, :] = attended
             dv_g = dv_g + mm(pb, jnp.where(in_lanes, da_g, zero))
-            dp = mm(v_g, jnp.where(in_rows, da_tg, zero))
+            dp = mm(v_g, rows_only(da_tg, h))
             row_term = jnp.sum(datt_t[at, :].astype(F32) * attended, axis=0, keepdims=True)
             ds = (p * (dp - row_term)).astype(BF16)
             dq_t[at, :] = mm(key_t[at, :], ds)
@@ -306,12 +319,12 @@
     out_ref[...] = mm(back, out_patch).astype(BF16)
 
 
-def patch(buf, w_qkv, w_proj, length):
+def patch(buf, w_qkv, w_proj, length, capacity):
     slots, channels = buf.shape[0], buf.shape[1] // 2
     group = 128
     groups = channels // group
     return pl.pallas_call(
-        patch_kernel,
+        functools.partial(patch_kernel, capacity),
         out_shape=(
             jax.ShapeDtypeStruct((slots, channels), BF16),
             jax.ShapeDtypeStruct((slots, channels), BF16),
@@ -386,6 +399,12 @@
         mine = (lax.axis_index("z"), lax.axis_index("x"), lax.axis_index("c"), lax.axis_index("rep"))
         rows = total.shape[0] // (nz * nx * nc)
         fine = gw_ref.shape[0] // (nz * nx * nc)
+        sxs = [lax.rem(x - mine[1] + nx, nx) for x in range(nx)]
+        sys = [lax.rem(y - mine[3] + nrep, nrep) for y in range(nrep)]
+        leads = [
+            [[sx * nrep + sy for sy in sys] for sx in sxs],
+            [[sy * nx + sx for sy in sys] for sx in sxs],
+        ]
         for core in range(nc):
             for is_mine, ref in ((True, keep_ref), (False, send_ref)):
                 same = mine[2] == core
@@ -397,11 +416,9 @@
                         four = lax.rem(z // 2 - lax.div(mine[0], 2) + nz // 2, nz // 2)
                         sz = pair * (nz // 2) + four
                         for x in range(nx):
-                            sx = lax.rem(x - mine[1] + nx, nx)
                             d = (z * nx + x) * nc + core
                             for part in range(PIECE // PART):
                                 half, y = part // nrep, part % nrep
-                                sy = lax.rem(y - mine[3] + nrep, nrep)
                                 first = part * PART
                                 if part == PIECE // PART - 1:
                                     terms = [
@@ -423,8 +440,7 @@
                                         ],
                                         axis=0,
                                     )
-                                lead = sx * nrep + sy if half == 0 else sy * nx + sx
-                                ref[half, lead, sz] = value.astype(BF16)
+                                ref[half, leads[half][x][y], sz] = value.astype(BF16)
 
 
 def grad_terms(slot, buf, g, gw, sizes):
@@ -562,7 +578,7 @@
     cot_buf, slot, own_t = pack_cot(serial, cotangent[0], feats, slots, capacity)
     nb = jnp.transpose(neighbours, (2, 0, 1))
     g, row_buf = gather_conv(nb, slot, cot_buf, below, own_t, above, feats, w_conv)
-    out_buf, dp_buf, gw = patch(exchange(row_buf), w_qkv, w_proj, length)
+    out_buf, dp_buf, gw = patch(exchange(row_buf), w_qkv, w_proj, length, capacity)
     keep, send = grad_terms(slot, exchange(dp_buf), g, gw, sizes)
 
     got = lax.ppermute(send, "c", [(0, 1), (1, 0)])

time: 188 us -> 186 us (0.989)
  no operation moved by 1% of the time
where the time goes in v2:
time: 186 us; the launch traced here: 184 us
  blocking collectives  61.2 us (33%)
  starting transfers between devices  53.4 us (29%)
  Pallas kernels  37.4 us (20%)
  waiting for transfers between devices  30.2 us (16%)
    all_to_all x2, blocking collectives, exchange(): out = lax.all_to_all(parts, SPACE, split_axis=0, concat_axis=0, tiled=True)  61.2 us
    ppermute x18, starting transfers between devices, shifted(): return lax.ppermute(a, axis, [(i, (i + by) % size) for i in range(size)])  40.5 us
    ppermute x18, waiting for transfers between devices, shifted(): return lax.ppermute(a, axis, [(i, (i + by) % size) for i in range(size)])  18.1 us
    pallas_call x1, Pallas kernels, patch(): pl.pallas_call(functools.partial(patch_kernel, capacity), out_shape=(jax....  13.6 us
    pallas_call x1, Pallas kernels, gather_conv(): pl.pallas_call(conv_kernel, grid=(steps + 1,), out_shape=(pltpu.HBM((coun...  13.5 us
    all_to_all x1, starting transfers between devices, exchange(): out = lax.all_to_all(parts, SPACE, split_axis=0, concat_axis=0, tiled=True)  6.61 us
    pallas_call x1, Pallas kernels, grad_terms(): pl.pallas_call(functools.partial(grad_kernel, sizes), grid=(GRAD_STEPS,),...  5.6 us
    ppermute x1, waiting for transfers between devices, per_device(): came = lax.ppermute(leave, 'z', [(i, i ^ 1) for i in range(nz)])  4.43 us
  transfers between devices with their start and end apart: 23, of which 12 were waited for; matrix products, arithmetic and copies ran while one was open for 0% of the time, Pallas kernels for 2%

profile of v2, /device:TPU:32, one launch (start us, length us, event | category | flops | bytes accessed | tf_op | source)
XLA Modules:
  0.0 183.8 jit_solution(2259534162386535886)
XLA Ops:
  0.6 0.9 slice_bitcast_fusion
  1.5 3.7 %collective-permute-start.1 = (bf16[128,256]{1,0:T(8,128)(2,1)S(1)}, bf16[128,256]{1,0:T(8,128)(2,1)S(1)}, u32[]{:S(2)}, u32[]{:S(2)}) collective-permute-start(bf16[128,256]{1,0:T(8,128)(2,1)S(1)} %get-tuple-element.92), channel_id=1, source_target_pairs={{4,0},{8,4},{12,8},{16,12},{20,16},{24,20},{28,24},{32,28},{36,32}... | collective-permute-start | bytes 196616 | tf_op jit(solution)/shard_map/ppermute | solution.py:577
  5.2 1.9 %collective-permute-start = (bf16[128,256]{1,0:T(8,128)(2,1)S(1)}, bf16[128,256]{1,0:T(8,128)(2,1)S(1)}, u32[]{:S(2)}, u32[]{:S(2)}) collective-permute-start(bf16[128,256]{1,0:T(8,128)(2,1)S(1)} %get-tuple-element.93), channel_id=1, source_target_pairs={{0,4},{4,8},{8,12},{12,16},{16,20},{20,24},{24,28},{28,32},{32,36}... | collective-permute-start | bytes 196616 | tf_op jit(solution)/shard_map/ppermute | solution.py:576
  7.1 1.8 %pack_cot.1 = (bf16[1024,256]{1,0:T(8,128)(2,1)S(1)}, f32[8,512]{1,0:T(8,128)S(1)}, bf16[256,512]{1,0:T(8,128)(2,1)S(1)}) custom-call(s32[1,512]{1,0:T(1,128)} %serial_ref.1, bf16[512,256]{1,0:T(8,128)(2,1)} %bitcast.50, bf16[512,256]{1,0:T(8,128)(2,1)} %bitcast.48), custom_call_target="tpu_custom_call" | custom-call | flops 268435456 | bytes 2097152 | tf_op jit(solution)/shard_map/pack_cot/pallas_call | solution.py:90
  9.0 0.0 collective-permute-done.1.above_ref
  9.0 3.9 %collective-permute-done.below_ref = bf16[128,256]{1,0:T(8,128)(2,1)S(1)} collective-permute-done((bf16[128,256]{1,0:T(8,128)(2,1)S(1)}, bf16[128,256]{1,0:T(8,128)(2,1)S(1)}, u32[]{:S(2)}, u32[]{:S(2)}) %collective-permute-start) | collective-permute-done | bytes 65568 | tf_op jit(solution)/shard_map/ppermute | solution.py:576
  12.9 13.5 %gather_conv.1 = (bf16[6912,512]{1,0:T(8,128)(2,1)}, bf16[1024,512]{1,0:T(8,128)(2,1)S(1)}) custom-call(s32[27,1,512]{2,1,0:T(1,128)} %bitcast.51, f32[8,512]{1,0:T(8,128)S(1)} %get-tuple-element.48.slot_ref, bf16[1024,256]{1,0:T(8,128)(2,1)S(1)} %get-tuple-element.49.cot_ref, bf16[128,256]{1,0:T(8,128)(2,1)S(1)} %collective-permute-done.below_ref, ...), custom_call_target="tpu_custom_call" | custom-call | flops 7247757312 | bytes 12582912 | tf_op jit(solution)/shard_map/gather_conv/pallas_call | solution.py:169
  26.4 0.0 copy-start
  26.4 0.0 copy-start.1
  26.4 38.2 %all_to_all.15 = bf16[64,16,512]{2,1,0:T(8,128)(2,1)S(1)} all-to-all(bf16[64,16,512]{2,1,0:T(8,128)(2,1)S(1)} %bitcast.32), channel_id=1, replica_groups=mesh['z'=8,'x'=4,'c'=2,'rep'=4] {'z','x','c'}, dimensions={0} | all-to-all | bytes 2097152 | tf_op jit(solution)/shard_map/all_to_all | solution.py:573
  64.5 0.0 copy-done
  64.6 0.0 copy-done.1
  64.6 13.6 %patch.1 = (bf16[1024,256]{1,0:T(8,128)(2,1)}, bf16[1024,256]{1,0:T(8,128)(2,1)S(1)}, f32[256,1024]{1,0:T(8,128)S(1)}) custom-call(bf16[1024,512]{1,0:T(8,128)(2,1)S(1)} %bitcast.33, bf16[256,768]{1,0:T(8,128)(2,1)S(1)} %copy-done, bf16[256,256]{1,0:T(8,128)(2,1)S(1)} %copy-done.1), custom_call_target="tpu_custom_call" | custom-call | flops 14000000000 | bytes 4194304 | tf_op jit(solution)/shard_map/patch/pallas_call | solution.py:326
  78.1 23.0 %all_to_all.16 = bf16[64,16,256]{2,1,0:T(8,128)(2,1)S(1)} all-to-all(bf16[64,16,256]{2,1,0:T(8,128)(2,1)S(1)} %bitcast.35), channel_id=1, replica_groups=mesh['z'=8,'x'=4,'c'=2,'rep'=4] {'z','x','c'}, dimensions={0} | all-to-all | bytes 1048576 | tf_op jit(solution)/shard_map/all_to_all | solution.py:573
  101.1 0.0 slice-done
  101.1 0.0 slice-done.1
  101.1 5.6 %grad_terms.1 = (bf16[2,16,8,16,256]{4,3,2,1,0:T(8,128)(2,1)S(1)}, bf16[2,16,8,16,256]{4,3,2,1,0:T(8,128)(2,1)S(1)}) custom-call(f32[8,512]{1,0:T(8,128)S(1)} %get-tuple-element.48.slot_ref, bf16[1024,256]{1,0:T(8,128)(2,1)S(1)} %bitcast.31, bf16[6912,512]{1,0:T(8,128)(2,1)S(1)} %bitcast.30, f32[256,1024]{1,0:T(8,128)S(1)} %get-tuple-element.54.gw_ref), custom_call_target="tpu_custom_call" | custom-call | flops 1811939328 | bytes 12582912 | tf_op jit(solution)/shard_map/grad_terms/pallas_call | solution.py:451
  106.7 0.6 collective-permute-start.2
  107.3 3.8 %collective-permute-done.2 = bf16[2,16,8,16,256]{4,3,2,1,0:T(8,128)(2,1)S(1)} collective-permute-done((bf16[2,16,8,16,256]{4,3,2,1,0:T(8,128)(2,1)S(1)}, bf16[2,16,8,16,256]{4,3,2,1,0:T(8,128)(2,1)S(1)}, u32[]{:S(2)}, u32[]{:S(2)}) %collective-permute-start.2) | collective-permute-done | bytes 2097184 | tf_op jit(solution)/shard_map/ppermute | solution.py:584
  111.1 0.5 add_up.4
  111.6 6.6 %all-to-all-start.2 = ((bf16[64,16,256]{2,1,0:T(8,128)(2,1)}), bf16[64,16,256]{2,1,0:T(8,128)(2,1)S(1)}, u32[]{:S(2)}, u32[]{:S(2)}) async-start(bf16[64,16,256]{2,1,0:T(8,128)(2,1)} %bitcast.11), calls=%async_computation.2 | async-start | bytes 1048576 | tf_op jit(solution)/shard_map/all_to_all | solution.py:573
  118.2 1.5 collective-permute-start.3
  119.7 2.7 %collective-permute-start.4 = (bf16[4,8,16,256]{3,2,1,0:T(8,128)(2,1)S(1)}, bf16[4,8,16,256]{3,2,1,0:T(8,128)(2,1)S(1)}, u32[]{:S(2)}, u32[]{:S(2)}) collective-permute-start(bf16[4,8,16,256]{3,2,1,0:T(8,128)(2,1)S(1)} %get-tuple-element.69), channel_id=1, source_target_pairs={{0,16},{8,24},{16,0},{24,8},{1,17},{9,25},{17,1},{25,9},{2,18},{10... | collective-permute-start | bytes 786440 | tf_op jit(solution)/shard_map/ppermute | solution.py:557
  122.4 1.5 collective-permute-start.5
  123.8 1.6 collective-permute-start.6
  125.4 2.9 %collective-permute-start.7 = (bf16[4,8,16,256]{3,2,1,0:T(8,128)(2,1)S(1)}, bf16[4,8,16,256]{3,2,1,0:T(8,128)(2,1)S(1)}, u32[]{:S(2)}, u32[]{:S(2)}) collective-permute-start(bf16[4,8,16,256]{3,2,1,0:T(8,128)(2,1)S(1)} %get-tuple-element.73), channel_id=1, source_target_pairs={{0,2},{1,3},{2,0},{3,1},{4,6},{5,7},{6,4},{7,5},{8,10},{9,11},{10,... | collective-permute-start | bytes 786440 | tf_op jit(solution)/shard_map/ppermute | solution.py:557
  128.3 5.0 %collective-permute-done.3.refs_1_ = bf16[4,8,16,256]{3,2,1,0:T(8,128)(2,1)S(1)} collective-permute-done((bf16[4,8,16,256]{3,2,1,0:T(8,128)(2,1)S(1)}, bf16[4,8,16,256]{3,2,1,0:T(8,128)(2,1)S(1)}, u32[]{:S(2)}, u32[]{:S(2)}) %collective-permute-start.3) | collective-permute-done | bytes 262176 | tf_op jit(solution)/shard_map/ppermute | solution.py:557
  133.3 3.0 %collective-permute-start.8 = (bf16[4,8,16,256]{3,2,1,0:T(8,128)(2,1)S(1)}, bf16[4,8,16,256]{3,2,1,0:T(8,128)(2,1)S(1)}, u32[]{:S(2)}, u32[]{:S(2)}) collective-permute-start(bf16[4,8,16,256]{3,2,1,0:T(8,128)(2,1)S(1)} %get-tuple-element.74), channel_id=1, source_target_pairs={{0,3},{1,0},{2,1},{3,2},{4,7},{5,4},{6,5},{7,6},{8,11},{9,8},{10,9... | collective-permute-start | bytes 786440 | tf_op jit(solution)/shard_map/ppermute | solution.py:557
  136.3 2.6 %collective-permute-done.4.refs_2_ = bf16[4,8,16,256]{3,2,1,0:T(8,128)(2,1)S(1)} collective-permute-done((bf16[4,8,16,256]{3,2,1,0:T(8,128)(2,1)S(1)}, bf16[4,8,16,256]{3,2,1,0:T(8,128)(2,1)S(1)}, u32[]{:S(2)}, u32[]{:S(2)}) %collective-permute-start.4) | collective-permute-done | bytes 262176 | tf_op jit(solution)/shard_map/ppermute | solution.py:557
  139.0 0.0 collective-permute-done.5.refs_3_
  139.0 0.0 collective-permute-done.6.refs_5_
  139.0 0.4 collective-permute-done.7.refs_6_
  139.4 1.3 collective-permute-done.8.refs_7_
  140.7 0.3 add_up.5
  140.9 1.1 collective-permute-start.9
  142.1 4.1 %collective-permute-start.10 = (bf16[1,8,16,256]{3,2,1,0:T(8,128)(2,1)S(1)}, bf16[1,8,16,256]{3,2,1,0:T(8,128)(2,1)S(1)}, u32[]{:S(2)}, u32[]{:S(2)}) collective-permute-start(bf16[1,8,16,256]{3,2,1,0:T(8,128)(2,1)S(1)} %get-tuple-element.77), channel_id=1, source_target_pairs={{0,2},{1,3},{2,0},{3,1},{4,6},{5,7},{6,4},{7,5},{8,10},{9,11},{10,... | collective-permute-start | bytes 196616 | tf_op jit(solution)/shard_map/ppermute | solution.py:557
  146.2 0.1 collective-permute-start.11
  146.3 0.2 collective-permute-start.12
  146.5 6.7 %collective-permute-start.13 = (bf16[1,8,16,256]{3,2,1,0:T(8,128)(2,1)S(1)}, bf16[1,8,16,256]{3,2,1,0:T(8,128)(2,1)S(1)}, u32[]{:S(2)}, u32[]{:S(2)}) collective-permute-start(bf16[1,8,16,256]{3,2,1,0:T(8,128)(2,1)S(1)} %get-tuple-element.81), channel_id=1, source_target_pairs={{0,16},{8,24},{16,0},{24,8},{1,17},{9,25},{17,1},{25,9},{2,18},{10... | collective-permute-start | bytes 196616 | tf_op jit(solution)/shard_map/ppermute | solution.py:557
  153.3 0.0 collective-permute-done.9
  153.3 2.6 %collective-permute-start.14 = (bf16[1,8,16,256]{3,2,1,0:T(8,128)(2,1)S(1)}, bf16[1,8,16,256]{3,2,1,0:T(8,128)(2,1)S(1)}, u32[]{:S(2)}, u32[]{:S(2)}) collective-permute-start(bf16[1,8,16,256]{3,2,1,0:T(8,128)(2,1)S(1)} %get-tuple-element.82), channel_id=1, source_target_pairs={{0,24},{8,0},{16,8},{24,16},{1,25},{9,1},{17,9},{25,17},{2,26},{10... | collective-permute-start | bytes 196616 | tf_op jit(solution)/shard_map/ppermute | solution.py:557
  155.9 0.0 collective-permute-done.10
  155.9 0.0 collective-permute-done.11
  155.9 0.0 collective-permute-done.12
  155.9 0.3 collective-permute-done.13
  156.2 1.6 collective-permute-done.14
  157.8 0.1 add_pairs.1
  157.9 0.1 collective-permute-start.15
  158.0 4.4 %collective-permute-done.15.refs_1_ = bf16[4,32,256]{2,1,0:T(8,128)(2,1)S(1)} collective-permute-done((bf16[4,32,256]{2,1,0:T(8,128)(2,1)S(1)}, bf16[4,32,256]{2,1,0:T(8,128)(2,1)S(1)}, u32[]{:S(2)}, u32[]{:S(2)}) %collective-permute-start.15) | collective-permute-done | bytes 65568 | tf_op jit(solution)/shard_map/ppermute | solution.py:609
  162.4 0.1 collective-permute-start.16
  162.5 5.2 %collective-permute-start.17 = (bf16[1,32,256]{2,1,0:T(8,128)(2,1)S(1)}, bf16[1,32,256]{2,1,0:T(8,128)(2,1)S(1)}, u32[]{:S(2)}, u32[]{:S(2)}) collective-permute-start(bf16[1,32,256]{2,1,0:T(8,128)(2,1)S(1)} %get-tuple-element.87), channel_id=1, source_target_pairs={{0,128},{32,160},{64,192},{96,224},{128,0},{160,32},{192,64},{224,... | collective-permute-start | bytes 49160 | tf_op jit(solution)/shard_map/ppermute | solution.py:557
  167.7 2.8 %collective-permute-start.18 = (bf16[1,32,256]{2,1,0:T(8,128)(2,1)S(1)}, bf16[1,32,256]{2,1,0:T(8,128)(2,1)S(1)}, u32[]{:S(2)}, u32[]{:S(2)}) collective-permute-start(bf16[1,32,256]{2,1,0:T(8,128)(2,1)S(1)} %get-tuple-element.88), channel_id=1, source_target_pairs={{0,192},{32,224},{64,0},{96,32},{128,64},{160,96},{192,128},{224,1... | collective-permute-start | bytes 49160 | tf_op jit(solution)/shard_map/ppermute | solution.py:557
  170.5 0.0 collective-permute-done.16.refs_1_
  170.5 0.0 collective-permute-done.17.refs_2_
  170.5 1.8 collective-permute-done.18.refs_3_
  172.4 0.6 collective-permute-start.21
  173.0 3.7 %collective-permute-start.20 = (bf16[32,256]{1,0:T(8,128)(2,1)S(1)}, bf16[32,256]{1,0:T(8,128)(2,1)S(1)}, u32[]{:S(2)}, u32[]{:S(2)}) collective-permute-start(bf16[32,256]{1,0:T(8,128)(2,1)S(1)} %bitcast.37), channel_id=1, source_target_pairs={{0,2},{1,3},{2,0},{3,1},{4,6},{5,7},{6,4},{7,5},{8,10},{9,11},{10,... | collective-permute-start | bytes 49160 | tf_op jit(solution)/shard_map/ppermute | solution.py:557
  176.7 0.0 collective-permute-start.19
  176.7 0.0 collective-permute-done.21.refs_3_
  176.7 1.7 collective-permute-done.20.refs_2_
  178.4 3.2 %collective-permute-done.19.refs_1_ = bf16[32,256]{1,0:T(8,128)(2,1)S(1)} collective-permute-done((bf16[32,256]{1,0:T(8,128)(2,1)S(1)}, bf16[32,256]{1,0:T(8,128)(2,1)S(1)}, u32[]{:S(2)}, u32[]{:S(2)}) %collective-permute-start.19) | collective-permute-done | bytes 16416 | tf_op jit(solution)/shard_map/ppermute | solution.py:557
  181.7 0.7 final.1
  182.3 0.0 all-to-all-done.2
  182.3 1.4 return_rows.1
  (5 shorter events, 0.0 us)
Async XLA Ops:
  1.5 7.4 %collective-permute-start.1 = (bf16[128,256]{1,0:T(8,128)(2,1)S(1)}, bf16[128,256]{1,0:T(8,128)(2,1)S(1)}, u32[]{:S(2)}, u32[]{:S(2)}) collective-permute-start(bf16[128,256]{1,0:T(8,128)(2,1)S(1)} %get-tuple-element.92), channel_id=1, source_target_pairs={{4,0},{8,4},{12,8},{16,12},{20,16},{24,20},{28,24},{32,28},{36,32}... | collective-permute-start | bytes 196616 | tf_op jit(solution)/shard_map/ppermute | solution.py:577
  5.2 7.7 %collective-permute-start = (bf16[128,256]{1,0:T(8,128)(2,1)S(1)}, bf16[128,256]{1,0:T(8,128)(2,1)S(1)}, u32[]{:S(2)}, u32[]{:S(2)}) collective-permute-start(bf16[128,256]{1,0:T(8,128)(2,1)S(1)} %get-tuple-element.93), channel_id=1, source_target_pairs={{0,4},{4,8},{8,12},{12,16},{16,20},{20,24},{24,28},{28,32},{32,36}... | collective-permute-start | bytes 196616 | tf_op jit(solution)/shard_map/ppermute | solution.py:576
  26.4 38.2 %copy-start = (bf16[256,768]{1,0:T(8,128)(2,1)S(1)}, bf16[256,768]{1,0:T(8,128)(2,1)}, u32[]{:S(2)}) copy-start(bf16[256,768]{1,0:T(8,128)(2,1)} %wqkv_ref.1) | copy-start | bytes 1179652
  26.4 38.2 %copy-start.1 = (bf16[256,256]{1,0:T(8,128)(2,1)S(1)}, bf16[256,256]{1,0:T(8,128)(2,1)}, u32[]{:S(2)}) copy-start(bf16[256,256]{1,0:T(8,128)(2,1)} %wproj_ref.1) | copy-start | bytes 393220
  64.5 36.6 %slice-start = ((s8[7077888]{0:T(1024)(128)(4,1)}), s8[4194304]{0:T(1024)(128)(4,1)S(1)}, s32[]{:S(2)}) async-start(s8[7077888]{0:T(1024)(128)(4,1)} %bitcast.29), calls=%async_computation.3 | async-start | bytes 8388608
  64.6 36.6 %slice-start.1 = ((s8[7077888]{0:T(1024)(128)(4,1)}), s8[2883584]{0:T(1024)(128)(4,1)S(1)}, s32[]{:S(2)}) async-start(s8[7077888]{0:T(1024)(128)(4,1)} %bitcast.29), calls=%async_computation.4 | async-start | bytes 5767168
  106.7 4.4 %collective-permute-start.2 = (bf16[2,16,8,16,256]{4,3,2,1,0:T(8,128)(2,1)S(1)}, bf16[2,16,8,16,256]{4,3,2,1,0:T(8,128)(2,1)S(1)}, u32[]{:S(2)}, u32[]{:S(2)}) collective-permute-start(bf16[2,16,8,16,256]{4,3,2,1,0:T(8,128)(2,1)S(1)} %get-tuple-element.56), channel_id=1, source_target_pairs={{0,4},{4,0},{1,5},{5,1},{2,6},{6,2},{3,7},{7,3},{8,12},{12,8},{9,1... | collective-permute-start | bytes 6291464 | tf_op jit(solution)/shard_map/ppermute | solution.py:584
  111.6 70.8 %all-to-all-start.2 = ((bf16[64,16,256]{2,1,0:T(8,128)(2,1)}), bf16[64,16,256]{2,1,0:T(8,128)(2,1)S(1)}, u32[]{:S(2)}, u32[]{:S(2)}) async-start(bf16[64,16,256]{2,1,0:T(8,128)(2,1)} %bitcast.11), calls=%async_computation.2 | async-start | bytes 1048576 | tf_op jit(solution)/shard_map/all_to_all | solution.py:573
  118.2 15.2 %collective-permute-start.3 = (bf16[4,8,16,256]{3,2,1,0:T(8,128)(2,1)S(1)}, bf16[4,8,16,256]{3,2,1,0:T(8,128)(2,1)S(1)}, u32[]{:S(2)}, u32[]{:S(2)}) collective-permute-start(bf16[4,8,16,256]{3,2,1,0:T(8,128)(2,1)S(1)} %get-tuple-element.68), channel_id=1, source_target_pairs={{0,8},{8,16},{16,24},{24,0},{1,9},{9,17},{17,25},{25,1},{2,10},{10... | collective-permute-start | bytes 786440 | tf_op jit(solution)/shard_map/ppermute | solution.py:557
  119.7 19.3 %collective-permute-start.4 = (bf16[4,8,16,256]{3,2,1,0:T(8,128)(2,1)S(1)}, bf16[4,8,16,256]{3,2,1,0:T(8,128)(2,1)S(1)}, u32[]{:S(2)}, u32[]{:S(2)}) collective-permute-start(bf16[4,8,16,256]{3,2,1,0:T(8,128)(2,1)S(1)} %get-tuple-element.69), channel_id=1, source_target_pairs={{0,16},{8,24},{16,0},{24,8},{1,17},{9,25},{17,1},{25,9},{2,18},{10... | collective-permute-start | bytes 786440 | tf_op jit(solution)/shard_map/ppermute | solution.py:557
  122.4 16.6 %collective-permute-start.5 = (bf16[4,8,16,256]{3,2,1,0:T(8,128)(2,1)S(1)}, bf16[4,8,16,256]{3,2,1,0:T(8,128)(2,1)S(1)}, u32[]{:S(2)}, u32[]{:S(2)}) collective-permute-start(bf16[4,8,16,256]{3,2,1,0:T(8,128)(2,1)S(1)} %get-tuple-element.70), channel_id=1, source_target_pairs={{0,24},{8,0},{16,8},{24,16},{1,25},{9,1},{17,9},{25,17},{2,26},{10... | collective-permute-start | bytes 786440 | tf_op jit(solution)/shard_map/ppermute | solution.py:557
  123.8 15.1 %collective-permute-start.6 = (bf16[4,8,16,256]{3,2,1,0:T(8,128)(2,1)S(1)}, bf16[4,8,16,256]{3,2,1,0:T(8,128)(2,1)S(1)}, u32[]{:S(2)}, u32[]{:S(2)}) collective-permute-start(bf16[4,8,16,256]{3,2,1,0:T(8,128)(2,1)S(1)} %get-tuple-element.72), channel_id=1, source_target_pairs={{0,1},{1,2},{2,3},{3,0},{4,5},{5,6},{6,7},{7,4},{8,9},{9,10},{10,1... | collective-permute-start | bytes 786440 | tf_op jit(solution)/shard_map/ppermute | solution.py:557
  125.4 14.0 %collective-permute-start.7 = (bf16[4,8,16,256]{3,2,1,0:T(8,128)(2,1)S(1)}, bf16[4,8,16,256]{3,2,1,0:T(8,128)(2,1)S(1)}, u32[]{:S(2)}, u32[]{:S(2)}) collective-permute-start(bf16[4,8,16,256]{3,2,1,0:T(8,128)(2,1)S(1)} %get-tuple-element.73), channel_id=1, source_target_pairs={{0,2},{1,3},{2,0},{3,1},{4,6},{5,7},{6,4},{7,5},{8,10},{9,11},{10,... | collective-permute-start | bytes 786440 | tf_op jit(solution)/shard_map/ppermute | solution.py:557
  133.3 7.3 %collective-permute-start.8 = (bf16[4,8,16,256]{3,2,1,0:T(8,128)(2,1)S(1)}, bf16[4,8,16,256]{3,2,1,0:T(8,128)(2,1)S(1)}, u32[]{:S(2)}, u32[]{:S(2)}) collective-permute-start(bf16[4,8,16,256]{3,2,1,0:T(8,128)(2,1)S(1)} %get-tuple-element.74), channel_id=1, source_target_pairs={{0,3},{1,0},{2,1},{3,2},{4,7},{5,4},{6,5},{7,6},{8,11},{9,8},{10,9... | collective-permute-start | bytes 786440 | tf_op jit(solution)/shard_map/ppermute | solution.py:557
  140.9 12.3 %collective-permute-start.9 = (bf16[1,8,16,256]{3,2,1,0:T(8,128)(2,1)S(1)}, bf16[1,8,16,256]{3,2,1,0:T(8,128)(2,1)S(1)}, u32[]{:S(2)}, u32[]{:S(2)}) collective-permute-start(bf16[1,8,16,256]{3,2,1,0:T(8,128)(2,1)S(1)} %get-tuple-element.76), channel_id=1, source_target_pairs={{0,1},{1,2},{2,3},{3,0},{4,5},{5,6},{6,7},{7,4},{8,9},{9,10},{10,1... | collective-permute-start | bytes 196616 | tf_op jit(solution)/shard_map/ppermute | solution.py:557
  142.1 13.8 %collective-permute-start.10 = (bf16[1,8,16,256]{3,2,1,0:T(8,128)(2,1)S(1)}, bf16[1,8,16,256]{3,2,1,0:T(8,128)(2,1)S(1)}, u32[]{:S(2)}, u32[]{:S(2)}) collective-permute-start(bf16[1,8,16,256]{3,2,1,0:T(8,128)(2,1)S(1)} %get-tuple-element.77), channel_id=1, source_target_pairs={{0,2},{1,3},{2,0},{3,1},{4,6},{5,7},{6,4},{7,5},{8,10},{9,11},{10,... | collective-permute-start | bytes 196616 | tf_op jit(solution)/shard_map/ppermute | solution.py:557
  146.2 9.7 %collective-permute-start.11 = (bf16[1,8,16,256]{3,2,1,0:T(8,128)(2,1)S(1)}, bf16[1,8,16,256]{3,2,1,0:T(8,128)(2,1)S(1)}, u32[]{:S(2)}, u32[]{:S(2)}) collective-permute-start(bf16[1,8,16,256]{3,2,1,0:T(8,128)(2,1)S(1)} %get-tuple-element.78), channel_id=1, source_target_pairs={{0,3},{1,0},{2,1},{3,2},{4,7},{5,4},{6,5},{7,6},{8,11},{9,8},{10,9... | collective-permute-start | bytes 196616 | tf_op jit(solution)/shard_map/ppermute | solution.py:557
  146.3 9.6 %collective-permute-start.12 = (bf16[1,8,16,256]{3,2,1,0:T(8,128)(2,1)S(1)}, bf16[1,8,16,256]{3,2,1,0:T(8,128)(2,1)S(1)}, u32[]{:S(2)}, u32[]{:S(2)}) collective-permute-start(bf16[1,8,16,256]{3,2,1,0:T(8,128)(2,1)S(1)} %get-tuple-element.80), channel_id=1, source_target_pairs={{0,8},{8,16},{16,24},{24,0},{1,9},{9,17},{17,25},{25,1},{2,10},{10... | collective-permute-start | bytes 196616 | tf_op jit(solution)/shard_map/ppermute | solution.py:557
  146.5 9.7 %collective-permute-start.13 = (bf16[1,8,16,256]{3,2,1,0:T(8,128)(2,1)S(1)}, bf16[1,8,16,256]{3,2,1,0:T(8,128)(2,1)S(1)}, u32[]{:S(2)}, u32[]{:S(2)}) collective-permute-start(bf16[1,8,16,256]{3,2,1,0:T(8,128)(2,1)S(1)} %get-tuple-element.81), channel_id=1, source_target_pairs={{0,16},{8,24},{16,0},{24,8},{1,17},{9,25},{17,1},{25,9},{2,18},{10... | collective-permute-start | bytes 196616 | tf_op jit(solution)/shard_map/ppermute | solution.py:557
  153.3 4.5 %collective-permute-start.14 = (bf16[1,8,16,256]{3,2,1,0:T(8,128)(2,1)S(1)}, bf16[1,8,16,256]{3,2,1,0:T(8,128)(2,1)S(1)}, u32[]{:S(2)}, u32[]{:S(2)}) collective-permute-start(bf16[1,8,16,256]{3,2,1,0:T(8,128)(2,1)S(1)} %get-tuple-element.82), channel_id=1, source_target_pairs={{0,24},{8,0},{16,8},{24,16},{1,25},{9,1},{17,9},{25,17},{2,26},{10... | collective-permute-start | bytes 196616 | tf_op jit(solution)/shard_map/ppermute | solution.py:557
  157.9 4.5 %collective-permute-start.15 = (bf16[4,32,256]{2,1,0:T(8,128)(2,1)S(1)}, bf16[4,32,256]{2,1,0:T(8,128)(2,1)S(1)}, u32[]{:S(2)}, u32[]{:S(2)}) collective-permute-start(bf16[4,32,256]{2,1,0:T(8,128)(2,1)S(1)} %get-tuple-element.84), channel_id=1, source_target_pairs={{0,32},{32,0},{64,96},{96,64},{128,160},{160,128},{192,224},{224,1... | collective-permute-start | bytes 196616 | tf_op jit(solution)/shard_map/ppermute | solution.py:609
  162.4 8.1 %collective-permute-start.16 = (bf16[1,32,256]{2,1,0:T(8,128)(2,1)S(1)}, bf16[1,32,256]{2,1,0:T(8,128)(2,1)S(1)}, u32[]{:S(2)}, u32[]{:S(2)}) collective-permute-start(bf16[1,32,256]{2,1,0:T(8,128)(2,1)S(1)} %get-tuple-element.86), channel_id=1, source_target_pairs={{0,64},{32,96},{64,128},{96,160},{128,192},{160,224},{192,0},{224,... | collective-permute-start | bytes 49160 | tf_op jit(solution)/shard_map/ppermute | solution.py:557
  162.5 8.0 %collective-permute-start.17 = (bf16[1,32,256]{2,1,0:T(8,128)(2,1)S(1)}, bf16[1,32,256]{2,1,0:T(8,128)(2,1)S(1)}, u32[]{:S(2)}, u32[]{:S(2)}) collective-permute-start(bf16[1,32,256]{2,1,0:T(8,128)(2,1)S(1)} %get-tuple-element.87), channel_id=1, source_target_pairs={{0,128},{32,160},{64,192},{96,224},{128,0},{160,32},{192,64},{224,... | collective-permute-start | bytes 49160 | tf_op jit(solution)/shard_map/ppermute | solution.py:557
  167.7 4.6 %collective-permute-start.18 = (bf16[1,32,256]{2,1,0:T(8,128)(2,1)S(1)}, bf16[1,32,256]{2,1,0:T(8,128)(2,1)S(1)}, u32[]{:S(2)}, u32[]{:S(2)}) collective-permute-start(bf16[1,32,256]{2,1,0:T(8,128)(2,1)S(1)} %get-tuple-element.88), channel_id=1, source_target_pairs={{0,192},{32,224},{64,0},{96,32},{128,64},{160,96},{192,128},{224,1... | collective-permute-start | bytes 49160 | tf_op jit(solution)/shard_map/ppermute | solution.py:557
  172.4 4.3 %collective-permute-start.21 = (bf16[32,256]{1,0:T(8,128)(2,1)S(1)}, bf16[32,256]{1,0:T(8,128)(2,1)S(1)}, u32[]{:S(2)}, u32[]{:S(2)}) collective-permute-start(bf16[32,256]{1,0:T(8,128)(2,1)S(1)} %bitcast.36), channel_id=1, source_target_pairs={{0,3},{1,0},{2,1},{3,2},{4,7},{5,4},{6,5},{7,6},{8,11},{9,8},{10,9... | collective-permute-start | bytes 49160 | tf_op jit(solution)/shard_map/ppermute | solution.py:557
  173.0 5.4 %collective-permute-start.20 = (bf16[32,256]{1,0:T(8,128)(2,1)S(1)}, bf16[32,256]{1,0:T(8,128)(2,1)S(1)}, u32[]{:S(2)}, u32[]{:S(2)}) collective-permute-start(bf16[32,256]{1,0:T(8,128)(2,1)S(1)} %bitcast.37), channel_id=1, source_target_pairs={{0,2},{1,3},{2,0},{3,1},{4,6},{5,7},{6,4},{7,5},{8,10},{9,11},{10,... | collective-permute-start | bytes 49160 | tf_op jit(solution)/shard_map/ppermute | solution.py:557
  176.7 4.9 %collective-permute-start.19 = (bf16[32,256]{1,0:T(8,128)(2,1)S(1)}, bf16[32,256]{1,0:T(8,128)(2,1)S(1)}, u32[]{:S(2)}, u32[]{:S(2)}) collective-permute-start(bf16[32,256]{1,0:T(8,128)(2,1)S(1)} %bitcast.38), channel_id=1, source_target_pairs={{0,1},{1,2},{2,3},{3,0},{4,5},{5,6},{6,7},{7,4},{8,9},{9,10},{10,1... | collective-permute-start | bytes 49160 | tf_op jit(solution)/shard_map/ppermute | solution.py:557

commit v3 on v2

--- a/solution.py
+++ b/solution.py
@@ -367,32 +367,25 @@
     )(slot, buf)
 
 
-GRAD_STEPS = 9
+GRAD_STEPS = 3
 PIECE = 128
 PART = 16
 
 
 def grad_kernel(
-    sizes, slot_ref, buf_ref, g_ref, gw_ref, keep_ref, send_ref, d_mixed, total, near, sems
+    sizes, slot_ref, buf_ref, g_ref, gw_ref, keep_ref, send_ref, d_mixed, total
 ):
     step = pl.program_id(0)
     nz, nx, nc, nrep = sizes
     block = g_ref.shape[0] // GRAD_STEPS
     channels = buf_ref.shape[1]
 
-    def fetch(i):
-        at = pl.ds(pl.multiple_of(i * block, block), block)
-        return pltpu.make_async_copy(g_ref.at[at, :], near.at[at, :], sems.at[i])
-
     @pl.when(step == 0)
     def _():
-        for i in range(GRAD_STEPS):
-            fetch(i).start()
         d_mixed[...] = unpack(slot_ref[...], buf_ref[...])
 
-    fetch(step).wait()
     at = pl.ds(pl.multiple_of(step * block, block), block)
-    total[at, :] = mm(near[at, :], d_mixed[...])
+    total[at, :] = mm(g_ref[at, :], d_mixed[...])
 
     @pl.when(step == pl.num_programs(0) - 1)
     def _():
@@ -455,15 +448,13 @@
         in_specs=[
             whole(8, length),
             whole(slots, channels),
-            pl.BlockSpec(memory_space=pltpu.HBM),
+            VMEM_SPEC,
             whole(*gw.shape),
         ],
         out_specs=(whole(*shape), whole(*shape)),
         scratch_shapes=[
             pltpu.VMEM((length, channels), BF16),
             pltpu.VMEM((g.shape[0], channels), F32),
-            pltpu.VMEM(g.shape, BF16),
-            pltpu.SemaphoreType.DMA((GRAD_STEPS,)),
         ],
         compiler_params=params(32, dimension_semantics=("arbitrary",)),
         cost_estimate=cost(2 * g.shape[0] * length * channels, 12 << 20),

time: 186 us -> 185 us (level)
  no operation moved by 1% of the time
where the time goes in v3:
time: 185 us; the launch traced here: 182 us
  blocking collectives  61.2 us (33%)
  starting transfers between devices  53.4 us (29%)
  Pallas kernels  35.8 us (19%)
  waiting for transfers between devices  30.2 us (16%)
    all_to_all x2, blocking collectives, exchange(): out = lax.all_to_all(parts, SPACE, split_axis=0, concat_axis=0, tiled=True)  61.2 us
    ppermute x18, starting transfers between devices, shifted(): return lax.ppermute(a, axis, [(i, (i + by) % size) for i in range(size)])  40.5 us
    ppermute x18, waiting for transfers between devices, shifted(): return lax.ppermute(a, axis, [(i, (i + by) % size) for i in range(size)])  18.1 us
    pallas_call x1, Pallas kernels, patch(): pl.pallas_call(functools.partial(patch_kernel, capacity), out_shape=(jax....  13.6 us
    pallas_call x1, Pallas kernels, gather_conv(): pl.pallas_call(conv_kernel, grid=(steps + 1,), out_shape=(pltpu.HBM((coun...  13.5 us
    all_to_all x1, starting transfers between devices, exchange(): out = lax.all_to_all(parts, SPACE, split_axis=0, concat_axis=0, tiled=True)  6.62 us
    ppermute x1, waiting for transfers between devices, per_device(): came = lax.ppermute(leave, 'z', [(i, i ^ 1) for i in range(nz)])  4.43 us
    pallas_call x1, Pallas kernels, grad_terms(): pl.pallas_call(functools.partial(grad_kernel, sizes), grid=(GRAD_STEPS,),...  3.97 us
  transfers between devices with their start and end apart: 23, of which 12 were waited for; matrix products, arithmetic and copies ran while one was open for 0% of the time, Pallas kernels for 2%

profile of v3, /device:TPU:32, one launch (start us, length us, event | category | flops | bytes accessed | tf_op | source)
XLA Modules:
  0.0 182.1 jit_solution(13167362443252342152)
XLA Ops:
  0.6 0.9 slice_bitcast_fusion
  1.5 3.7 %collective-permute-start.1 = (bf16[128,256]{1,0:T(8,128)(2,1)S(1)}, bf16[128,256]{1,0:T(8,128)(2,1)S(1)}, u32[]{:S(2)}, u32[]{:S(2)}) collective-permute-start(bf16[128,256]{1,0:T(8,128)(2,1)S(1)} %get-tuple-element.92), channel_id=1, source_target_pairs={{4,0},{8,4},{12,8},{16,12},{20,16},{24,20},{28,24},{32,28},{36,32}... | collective-permute-start | bytes 196616 | tf_op jit(solution)/shard_map/ppermute | solution.py:568
  5.2 1.9 %collective-permute-start = (bf16[128,256]{1,0:T(8,128)(2,1)S(1)}, bf16[128,256]{1,0:T(8,128)(2,1)S(1)}, u32[]{:S(2)}, u32[]{:S(2)}) collective-permute-start(bf16[128,256]{1,0:T(8,128)(2,1)S(1)} %get-tuple-element.93), channel_id=1, source_target_pairs={{0,4},{4,8},{8,12},{12,16},{16,20},{20,24},{24,28},{28,32},{32,36}... | collective-permute-start | bytes 196616 | tf_op jit(solution)/shard_map/ppermute | solution.py:567
  7.1 1.8 %pack_cot.1 = (bf16[1024,256]{1,0:T(8,128)(2,1)S(1)}, f32[8,512]{1,0:T(8,128)S(1)}, bf16[256,512]{1,0:T(8,128)(2,1)S(1)}) custom-call(s32[1,512]{1,0:T(1,128)} %serial_ref.1, bf16[512,256]{1,0:T(8,128)(2,1)} %bitcast.50, bf16[512,256]{1,0:T(8,128)(2,1)} %bitcast.48), custom_call_target="tpu_custom_call" | custom-call | flops 268435456 | bytes 2097152 | tf_op jit(solution)/shard_map/pack_cot/pallas_call | solution.py:90
  9.0 0.0 collective-permute-done.1.above_ref
  9.0 3.9 %collective-permute-done.below_ref = bf16[128,256]{1,0:T(8,128)(2,1)S(1)} collective-permute-done((bf16[128,256]{1,0:T(8,128)(2,1)S(1)}, bf16[128,256]{1,0:T(8,128)(2,1)S(1)}, u32[]{:S(2)}, u32[]{:S(2)}) %collective-permute-start) | collective-permute-done | bytes 65568 | tf_op jit(solution)/shard_map/ppermute | solution.py:567
  12.9 13.5 %gather_conv.1 = (bf16[6912,512]{1,0:T(8,128)(2,1)}, bf16[1024,512]{1,0:T(8,128)(2,1)S(1)}) custom-call(s32[27,1,512]{2,1,0:T(1,128)} %bitcast.51, f32[8,512]{1,0:T(8,128)S(1)} %get-tuple-element.48.slot_ref, bf16[1024,256]{1,0:T(8,128)(2,1)S(1)} %get-tuple-element.49.cot_ref, bf16[128,256]{1,0:T(8,128)(2,1)S(1)} %collective-permute-done.below_ref, ...), custom_call_target="tpu_custom_call" | custom-call | flops 7247757312 | bytes 12582912 | tf_op jit(solution)/shard_map/gather_conv/pallas_call | solution.py:169
  26.4 0.0 copy-start
  26.4 0.0 copy-start.1
  26.4 38.2 %all_to_all.15 = bf16[64,16,512]{2,1,0:T(8,128)(2,1)S(1)} all-to-all(bf16[64,16,512]{2,1,0:T(8,128)(2,1)S(1)} %bitcast.32), channel_id=1, replica_groups=mesh['z'=8,'x'=4,'c'=2,'rep'=4] {'z','x','c'}, dimensions={0} | all-to-all | bytes 2097152 | tf_op jit(solution)/shard_map/all_to_all | solution.py:564
  64.5 0.0 copy-done
  64.6 0.0 copy-done.1
  64.6 13.6 %patch.1 = (bf16[1024,256]{1,0:T(8,128)(2,1)}, bf16[1024,256]{1,0:T(8,128)(2,1)S(1)}, f32[256,1024]{1,0:T(8,128)S(1)}) custom-call(bf16[1024,512]{1,0:T(8,128)(2,1)S(1)} %bitcast.33, bf16[256,768]{1,0:T(8,128)(2,1)S(1)} %copy-done, bf16[256,256]{1,0:T(8,128)(2,1)S(1)} %copy-done.1), custom_call_target="tpu_custom_call" | custom-call | flops 14000000000 | bytes 4194304 | tf_op jit(solution)/shard_map/patch/pallas_call | solution.py:326
  78.1 23.0 %all_to_all.16 = bf16[64,16,256]{2,1,0:T(8,128)(2,1)S(1)} all-to-all(bf16[64,16,256]{2,1,0:T(8,128)(2,1)S(1)} %bitcast.35), channel_id=1, replica_groups=mesh['z'=8,'x'=4,'c'=2,'rep'=4] {'z','x','c'}, dimensions={0} | all-to-all | bytes 1048576 | tf_op jit(solution)/shard_map/all_to_all | solution.py:564
  101.1 0.0 slice-done
  101.1 0.0 slice-done.1
  101.1 4.0 %grad_terms.1 = (bf16[2,16,8,16,256]{4,3,2,1,0:T(8,128)(2,1)S(1)}, bf16[2,16,8,16,256]{4,3,2,1,0:T(8,128)(2,1)S(1)}) custom-call(f32[8,512]{1,0:T(8,128)S(1)} %get-tuple-element.48.slot_ref, bf16[1024,256]{1,0:T(8,128)(2,1)S(1)} %bitcast.31, bf16[6912,512]{1,0:T(8,128)(2,1)S(1)} %bitcast.30, f32[256,1024]{1,0:T(8,128)S(1)} %get-tuple-element.54.gw_ref), custom_call_target="tpu_custom_call" | custom-call | flops 1811939328 | bytes 12582912 | tf_op jit(solution)/shard_map/grad_terms/pallas_call | solution.py:444
  105.1 0.6 collective-permute-start.2
  105.7 3.8 %collective-permute-done.2 = bf16[2,16,8,16,256]{4,3,2,1,0:T(8,128)(2,1)S(1)} collective-permute-done((bf16[2,16,8,16,256]{4,3,2,1,0:T(8,128)(2,1)S(1)}, bf16[2,16,8,16,256]{4,3,2,1,0:T(8,128)(2,1)S(1)}, u32[]{:S(2)}, u32[]{:S(2)}) %collective-permute-start.2) | collective-permute-done | bytes 2097184 | tf_op jit(solution)/shard_map/ppermute | solution.py:575
  109.4 0.5 add_up.4
  109.9 6.6 %all-to-all-start.2 = ((bf16[64,16,256]{2,1,0:T(8,128)(2,1)}), bf16[64,16,256]{2,1,0:T(8,128)(2,1)S(1)}, u32[]{:S(2)}, u32[]{:S(2)}) async-start(bf16[64,16,256]{2,1,0:T(8,128)(2,1)} %bitcast.11), calls=%async_computation.2 | async-start | bytes 1048576 | tf_op jit(solution)/shard_map/all_to_all | solution.py:564
  116.5 1.5 collective-permute-start.3
  118.1 2.7 %collective-permute-start.4 = (bf16[4,8,16,256]{3,2,1,0:T(8,128)(2,1)S(1)}, bf16[4,8,16,256]{3,2,1,0:T(8,128)(2,1)S(1)}, u32[]{:S(2)}, u32[]{:S(2)}) collective-permute-start(bf16[4,8,16,256]{3,2,1,0:T(8,128)(2,1)S(1)} %get-tuple-element.69), channel_id=1, source_target_pairs={{0,16},{8,24},{16,0},{24,8},{1,17},{9,25},{17,1},{25,9},{2,18},{10... | collective-permute-start | bytes 786440 | tf_op jit(solution)/shard_map/ppermute | solution.py:548
  120.8 1.5 collective-permute-start.5
  122.2 1.6 collective-permute-start.6
  123.8 2.9 %collective-permute-start.7 = (bf16[4,8,16,256]{3,2,1,0:T(8,128)(2,1)S(1)}, bf16[4,8,16,256]{3,2,1,0:T(8,128)(2,1)S(1)}, u32[]{:S(2)}, u32[]{:S(2)}) collective-permute-start(bf16[4,8,16,256]{3,2,1,0:T(8,128)(2,1)S(1)} %get-tuple-element.73), channel_id=1, source_target_pairs={{0,2},{1,3},{2,0},{3,1},{4,6},{5,7},{6,4},{7,5},{8,10},{9,11},{10,... | collective-permute-start | bytes 786440 | tf_op jit(solution)/shard_map/ppermute | solution.py:548
  126.7 5.0 %collective-permute-done.3.refs_1_ = bf16[4,8,16,256]{3,2,1,0:T(8,128)(2,1)S(1)} collective-permute-done((bf16[4,8,16,256]{3,2,1,0:T(8,128)(2,1)S(1)}, bf16[4,8,16,256]{3,2,1,0:T(8,128)(2,1)S(1)}, u32[]{:S(2)}, u32[]{:S(2)}) %collective-permute-start.3) | collective-permute-done | bytes 262176 | tf_op jit(solution)/shard_map/ppermute | solution.py:548
  131.7 3.0 %collective-permute-start.8 = (bf16[4,8,16,256]{3,2,1,0:T(8,128)(2,1)S(1)}, bf16[4,8,16,256]{3,2,1,0:T(8,128)(2,1)S(1)}, u32[]{:S(2)}, u32[]{:S(2)}) collective-permute-start(bf16[4,8,16,256]{3,2,1,0:T(8,128)(2,1)S(1)} %get-tuple-element.74), channel_id=1, source_target_pairs={{0,3},{1,0},{2,1},{3,2},{4,7},{5,4},{6,5},{7,6},{8,11},{9,8},{10,9... | collective-permute-start | bytes 786440 | tf_op jit(solution)/shard_map/ppermute | solution.py:548
  134.7 2.6 %collective-permute-done.4.refs_2_ = bf16[4,8,16,256]{3,2,1,0:T(8,128)(2,1)S(1)} collective-permute-done((bf16[4,8,16,256]{3,2,1,0:T(8,128)(2,1)S(1)}, bf16[4,8,16,256]{3,2,1,0:T(8,128)(2,1)S(1)}, u32[]{:S(2)}, u32[]{:S(2)}) %collective-permute-start.4) | collective-permute-done | bytes 262176 | tf_op jit(solution)/shard_map/ppermute | solution.py:548
  137.4 0.0 collective-permute-done.5.refs_3_
  137.4 0.0 collective-permute-done.6.refs_5_
  137.4 0.4 collective-permute-done.7.refs_6_
  137.8 1.3 collective-permute-done.8.refs_7_
  139.1 0.3 add_up.5
  139.3 1.1 collective-permute-start.9
  140.5 4.1 %collective-permute-start.10 = (bf16[1,8,16,256]{3,2,1,0:T(8,128)(2,1)S(1)}, bf16[1,8,16,256]{3,2,1,0:T(8,128)(2,1)S(1)}, u32[]{:S(2)}, u32[]{:S(2)}) collective-permute-start(bf16[1,8,16,256]{3,2,1,0:T(8,128)(2,1)S(1)} %get-tuple-element.77), channel_id=1, source_target_pairs={{0,2},{1,3},{2,0},{3,1},{4,6},{5,7},{6,4},{7,5},{8,10},{9,11},{10,... | collective-permute-start | bytes 196616 | tf_op jit(solution)/shard_map/ppermute | solution.py:548
  144.5 0.1 collective-permute-start.11
  144.7 0.2 collective-permute-start.12
  144.9 6.7 %collective-permute-start.13 = (bf16[1,8,16,256]{3,2,1,0:T(8,128)(2,1)S(1)}, bf16[1,8,16,256]{3,2,1,0:T(8,128)(2,1)S(1)}, u32[]{:S(2)}, u32[]{:S(2)}) collective-permute-start(bf16[1,8,16,256]{3,2,1,0:T(8,128)(2,1)S(1)} %get-tuple-element.81), channel_id=1, source_target_pairs={{0,16},{8,24},{16,0},{24,8},{1,17},{9,25},{17,1},{25,9},{2,18},{10... | collective-permute-start | bytes 196616 | tf_op jit(solution)/shard_map/ppermute | solution.py:548
  151.7 0.0 collective-permute-done.9
  151.7 2.6 %collective-permute-start.14 = (bf16[1,8,16,256]{3,2,1,0:T(8,128)(2,1)S(1)}, bf16[1,8,16,256]{3,2,1,0:T(8,128)(2,1)S(1)}, u32[]{:S(2)}, u32[]{:S(2)}) collective-permute-start(bf16[1,8,16,256]{3,2,1,0:T(8,128)(2,1)S(1)} %get-tuple-element.82), channel_id=1, source_target_pairs={{0,24},{8,0},{16,8},{24,16},{1,25},{9,1},{17,9},{25,17},{2,26},{10... | collective-permute-start | bytes 196616 | tf_op jit(solution)/shard_map/ppermute | solution.py:548
  154.3 0.0 collective-permute-done.10
  154.3 0.0 collective-permute-done.11
  154.3 0.0 collective-permute-done.12
  154.3 0.3 collective-permute-done.13
  154.6 1.6 collective-permute-done.14
  156.2 0.1 add_pairs.1
  156.3 0.1 collective-permute-start.15
  156.4 4.4 %collective-permute-done.15.refs_1_ = bf16[4,32,256]{2,1,0:T(8,128)(2,1)S(1)} collective-permute-done((bf16[4,32,256]{2,1,0:T(8,128)(2,1)S(1)}, bf16[4,32,256]{2,1,0:T(8,128)(2,1)S(1)}, u32[]{:S(2)}, u32[]{:S(2)}) %collective-permute-start.15) | collective-permute-done | bytes 65568 | tf_op jit(solution)/shard_map/ppermute | solution.py:600
  160.8 0.1 collective-permute-start.16
  160.9 5.2 %collective-permute-start.17 = (bf16[1,32,256]{2,1,0:T(8,128)(2,1)S(1)}, bf16[1,32,256]{2,1,0:T(8,128)(2,1)S(1)}, u32[]{:S(2)}, u32[]{:S(2)}) collective-permute-start(bf16[1,32,256]{2,1,0:T(8,128)(2,1)S(1)} %get-tuple-element.87), channel_id=1, source_target_pairs={{0,128},{32,160},{64,192},{96,224},{128,0},{160,32},{192,64},{224,... | collective-permute-start | bytes 49160 | tf_op jit(solution)/shard_map/ppermute | solution.py:548
  166.1 2.8 %collective-permute-start.18 = (bf16[1,32,256]{2,1,0:T(8,128)(2,1)S(1)}, bf16[1,32,256]{2,1,0:T(8,128)(2,1)S(1)}, u32[]{:S(2)}, u32[]{:S(2)}) collective-permute-start(bf16[1,32,256]{2,1,0:T(8,128)(2,1)S(1)} %get-tuple-element.88), channel_id=1, source_target_pairs={{0,192},{32,224},{64,0},{96,32},{128,64},{160,96},{192,128},{224,1... | collective-permute-start | bytes 49160 | tf_op jit(solution)/shard_map/ppermute | solution.py:548
  168.9 0.0 collective-permute-done.16.refs_1_
  168.9 0.0 collective-permute-done.17.refs_2_
  168.9 1.8 %collective-permute-done.18.refs_3_ = bf16[1,32,256]{2,1,0:T(8,128)(2,1)S(1)} collective-permute-done((bf16[1,32,256]{2,1,0:T(8,128)(2,1)S(1)}, bf16[1,32,256]{2,1,0:T(8,128)(2,1)S(1)}, u32[]{:S(2)}, u32[]{:S(2)}) %collective-permute-start.18) | collective-permute-done | bytes 16416 | tf_op jit(solution)/shard_map/ppermute | solution.py:548
  170.7 0.6 collective-permute-start.21
  171.4 3.7 %collective-permute-start.20 = (bf16[32,256]{1,0:T(8,128)(2,1)S(1)}, bf16[32,256]{1,0:T(8,128)(2,1)S(1)}, u32[]{:S(2)}, u32[]{:S(2)}) collective-permute-start(bf16[32,256]{1,0:T(8,128)(2,1)S(1)} %bitcast.37), channel_id=1, source_target_pairs={{0,2},{1,3},{2,0},{3,1},{4,6},{5,7},{6,4},{7,5},{8,10},{9,11},{10,... | collective-permute-start | bytes 49160 | tf_op jit(solution)/shard_map/ppermute | solution.py:548
  175.1 0.0 collective-permute-start.19
  175.1 0.0 collective-permute-done.21.refs_3_
  175.1 1.7 collective-permute-done.20.refs_2_
  176.8 3.2 %collective-permute-done.19.refs_1_ = bf16[32,256]{1,0:T(8,128)(2,1)S(1)} collective-permute-done((bf16[32,256]{1,0:T(8,128)(2,1)S(1)}, bf16[32,256]{1,0:T(8,128)(2,1)S(1)}, u32[]{:S(2)}, u32[]{:S(2)}) %collective-permute-start.19) | collective-permute-done | bytes 16416 | tf_op jit(solution)/shard_map/ppermute | solution.py:548
  180.0 0.7 final.1
  180.7 0.0 all-to-all-done.2
  180.7 1.4 return_rows.1
  (5 shorter events, 0.0 us)
Async XLA Ops:
  1.5 7.4 %collective-permute-start.1 = (bf16[128,256]{1,0:T(8,128)(2,1)S(1)}, bf16[128,256]{1,0:T(8,128)(2,1)S(1)}, u32[]{:S(2)}, u32[]{:S(2)}) collective-permute-start(bf16[128,256]{1,0:T(8,128)(2,1)S(1)} %get-tuple-element.92), channel_id=1, source_target_pairs={{4,0},{8,4},{12,8},{16,12},{20,16},{24,20},{28,24},{32,28},{36,32}... | collective-permute-start | bytes 196616 | tf_op jit(solution)/shard_map/ppermute | solution.py:568
  5.2 7.7 %collective-permute-start = (bf16[128,256]{1,0:T(8,128)(2,1)S(1)}, bf16[128,256]{1,0:T(8,128)(2,1)S(1)}, u32[]{:S(2)}, u32[]{:S(2)}) collective-permute-start(bf16[128,256]{1,0:T(8,128)(2,1)S(1)} %get-tuple-element.93), channel_id=1, source_target_pairs={{0,4},{4,8},{8,12},{12,16},{16,20},{20,24},{24,28},{28,32},{32,36}... | collective-permute-start | bytes 196616 | tf_op jit(solution)/shard_map/ppermute | solution.py:567
  26.4 38.2 %copy-start = (bf16[256,768]{1,0:T(8,128)(2,1)S(1)}, bf16[256,768]{1,0:T(8,128)(2,1)}, u32[]{:S(2)}) copy-start(bf16[256,768]{1,0:T(8,128)(2,1)} %wqkv_ref.1) | copy-start | bytes 1179652
  26.4 38.2 %copy-start.1 = (bf16[256,256]{1,0:T(8,128)(2,1)S(1)}, bf16[256,256]{1,0:T(8,128)(2,1)}, u32[]{:S(2)}) copy-start(bf16[256,256]{1,0:T(8,128)(2,1)} %wproj_ref.1) | copy-start | bytes 393220
  64.5 36.6 %slice-start = ((s8[7077888]{0:T(1024)(128)(4,1)}), s8[4194304]{0:T(1024)(128)(4,1)S(1)}, s32[]{:S(2)}) async-start(s8[7077888]{0:T(1024)(128)(4,1)} %bitcast.29), calls=%async_computation.3 | async-start | bytes 8388608
  64.6 36.6 %slice-start.1 = ((s8[7077888]{0:T(1024)(128)(4,1)}), s8[2883584]{0:T(1024)(128)(4,1)S(1)}, s32[]{:S(2)}) async-start(s8[7077888]{0:T(1024)(128)(4,1)} %bitcast.29), calls=%async_computation.4 | async-start | bytes 5767168
  105.1 4.4 %collective-permute-start.2 = (bf16[2,16,8,16,256]{4,3,2,1,0:T(8,128)(2,1)S(1)}, bf16[2,16,8,16,256]{4,3,2,1,0:T(8,128)(2,1)S(1)}, u32[]{:S(2)}, u32[]{:S(2)}) collective-permute-start(bf16[2,16,8,16,256]{4,3,2,1,0:T(8,128)(2,1)S(1)} %get-tuple-element.56), channel_id=1, source_target_pairs={{0,4},{4,0},{1,5},{5,1},{2,6},{6,2},{3,7},{7,3},{8,12},{12,8},{9,1... | collective-permute-start | bytes 6291464 | tf_op jit(solution)/shard_map/ppermute | solution.py:575
  109.9 70.8 %all-to-all-start.2 = ((bf16[64,16,256]{2,1,0:T(8,128)(2,1)}), bf16[64,16,256]{2,1,0:T(8,128)(2,1)S(1)}, u32[]{:S(2)}, u32[]{:S(2)}) async-start(bf16[64,16,256]{2,1,0:T(8,128)(2,1)} %bitcast.11), calls=%async_computation.2 | async-start | bytes 1048576 | tf_op jit(solution)/shard_map/all_to_all | solution.py:564
  116.5 15.2 %collective-permute-start.3 = (bf16[4,8,16,256]{3,2,1,0:T(8,128)(2,1)S(1)}, bf16[4,8,16,256]{3,2,1,0:T(8,128)(2,1)S(1)}, u32[]{:S(2)}, u32[]{:S(2)}) collective-permute-start(bf16[4,8,16,256]{3,2,1,0:T(8,128)(2,1)S(1)} %get-tuple-element.68), channel_id=1, source_target_pairs={{0,8},{8,16},{16,24},{24,0},{1,9},{9,17},{17,25},{25,1},{2,10},{10... | collective-permute-start | bytes 786440 | tf_op jit(solution)/shard_map/ppermute | solution.py:548
  118.1 19.3 %collective-permute-start.4 = (bf16[4,8,16,256]{3,2,1,0:T(8,128)(2,1)S(1)}, bf16[4,8,16,256]{3,2,1,0:T(8,128)(2,1)S(1)}, u32[]{:S(2)}, u32[]{:S(2)}) collective-permute-start(bf16[4,8,16,256]{3,2,1,0:T(8,128)(2,1)S(1)} %get-tuple-element.69), channel_id=1, source_target_pairs={{0,16},{8,24},{16,0},{24,8},{1,17},{9,25},{17,1},{25,9},{2,18},{10... | collective-permute-start | bytes 786440 | tf_op jit(solution)/shard_map/ppermute | solution.py:548
  120.8 16.6 %collective-permute-start.5 = (bf16[4,8,16,256]{3,2,1,0:T(8,128)(2,1)S(1)}, bf16[4,8,16,256]{3,2,1,0:T(8,128)(2,1)S(1)}, u32[]{:S(2)}, u32[]{:S(2)}) collective-permute-start(bf16[4,8,16,256]{3,2,1,0:T(8,128)(2,1)S(1)} %get-tuple-element.70), channel_id=1, source_target_pairs={{0,24},{8,0},{16,8},{24,16},{1,25},{9,1},{17,9},{25,17},{2,26},{10... | collective-permute-start | bytes 786440 | tf_op jit(solution)/shard_map/ppermute | solution.py:548
  122.2 15.1 %collective-permute-start.6 = (bf16[4,8,16,256]{3,2,1,0:T(8,128)(2,1)S(1)}, bf16[4,8,16,256]{3,2,1,0:T(8,128)(2,1)S(1)}, u32[]{:S(2)}, u32[]{:S(2)}) collective-permute-start(bf16[4,8,16,256]{3,2,1,0:T(8,128)(2,1)S(1)} %get-tuple-element.72), channel_id=1, source_target_pairs={{0,1},{1,2},{2,3},{3,0},{4,5},{5,6},{6,7},{7,4},{8,9},{9,10},{10,1... | collective-permute-start | bytes 786440 | tf_op jit(solution)/shard_map/ppermute | solution.py:548
  123.8 14.0 %collective-permute-start.7 = (bf16[4,8,16,256]{3,2,1,0:T(8,128)(2,1)S(1)}, bf16[4,8,16,256]{3,2,1,0:T(8,128)(2,1)S(1)}, u32[]{:S(2)}, u32[]{:S(2)}) collective-permute-start(bf16[4,8,16,256]{3,2,1,0:T(8,128)(2,1)S(1)} %get-tuple-element.73), channel_id=1, source_target_pairs={{0,2},{1,3},{2,0},{3,1},{4,6},{5,7},{6,4},{7,5},{8,10},{9,11},{10,... | collective-permute-start | bytes 786440 | tf_op jit(solution)/shard_map/ppermute | solution.py:548
  131.7 7.3 %collective-permute-start.8 = (bf16[4,8,16,256]{3,2,1,0:T(8,128)(2,1)S(1)}, bf16[4,8,16,256]{3,2,1,0:T(8,128)(2,1)S(1)}, u32[]{:S(2)}, u32[]{:S(2)}) collective-permute-start(bf16[4,8,16,256]{3,2,1,0:T(8,128)(2,1)S(1)} %get-tuple-element.74), channel_id=1, source_target_pairs={{0,3},{1,0},{2,1},{3,2},{4,7},{5,4},{6,5},{7,6},{8,11},{9,8},{10,9... | collective-permute-start | bytes 786440 | tf_op jit(solution)/shard_map/ppermute | solution.py:548
  139.3 12.3 %collective-permute-start.9 = (bf16[1,8,16,256]{3,2,1,0:T(8,128)(2,1)S(1)}, bf16[1,8,16,256]{3,2,1,0:T(8,128)(2,1)S(1)}, u32[]{:S(2)}, u32[]{:S(2)}) collective-permute-start(bf16[1,8,16,256]{3,2,1,0:T(8,128)(2,1)S(1)} %get-tuple-element.76), channel_id=1, source_target_pairs={{0,1},{1,2},{2,3},{3,0},{4,5},{5,6},{6,7},{7,4},{8,9},{9,10},{10,1... | collective-permute-start | bytes 196616 | tf_op jit(solution)/shard_map/ppermute | solution.py:548
  140.5 13.8 %collective-permute-start.10 = (bf16[1,8,16,256]{3,2,1,0:T(8,128)(2,1)S(1)}, bf16[1,8,16,256]{3,2,1,0:T(8,128)(2,1)S(1)}, u32[]{:S(2)}, u32[]{:S(2)}) collective-permute-start(bf16[1,8,16,256]{3,2,1,0:T(8,128)(2,1)S(1)} %get-tuple-element.77), channel_id=1, source_target_pairs={{0,2},{1,3},{2,0},{3,1},{4,6},{5,7},{6,4},{7,5},{8,10},{9,11},{10,... | collective-permute-start | bytes 196616 | tf_op jit(solution)/shard_map/ppermute | solution.py:548
  144.5 9.7 %collective-permute-start.11 = (bf16[1,8,16,256]{3,2,1,0:T(8,128)(2,1)S(1)}, bf16[1,8,16,256]{3,2,1,0:T(8,128)(2,1)S(1)}, u32[]{:S(2)}, u32[]{:S(2)}) collective-permute-start(bf16[1,8,16,256]{3,2,1,0:T(8,128)(2,1)S(1)} %get-tuple-element.78), channel_id=1, source_target_pairs={{0,3},{1,0},{2,1},{3,2},{4,7},{5,4},{6,5},{7,6},{8,11},{9,8},{10,9... | collective-permute-start | bytes 196616 | tf_op jit(solution)/shard_map/ppermute | solution.py:548
  144.7 9.6 %collective-permute-start.12 = (bf16[1,8,16,256]{3,2,1,0:T(8,128)(2,1)S(1)}, bf16[1,8,16,256]{3,2,1,0:T(8,128)(2,1)S(1)}, u32[]{:S(2)}, u32[]{:S(2)}) collective-permute-start(bf16[1,8,16,256]{3,2,1,0:T(8,128)(2,1)S(1)} %get-tuple-element.80), channel_id=1, source_target_pairs={{0,8},{8,16},{16,24},{24,0},{1,9},{9,17},{17,25},{25,1},{2,10},{10... | collective-permute-start | bytes 196616 | tf_op jit(solution)/shard_map/ppermute | solution.py:548
  144.9 9.7 %collective-permute-start.13 = (bf16[1,8,16,256]{3,2,1,0:T(8,128)(2,1)S(1)}, bf16[1,8,16,256]{3,2,1,0:T(8,128)(2,1)S(1)}, u32[]{:S(2)}, u32[]{:S(2)}) collective-permute-start(bf16[1,8,16,256]{3,2,1,0:T(8,128)(2,1)S(1)} %get-tuple-element.81), channel_id=1, source_target_pairs={{0,16},{8,24},{16,0},{24,8},{1,17},{9,25},{17,1},{25,9},{2,18},{10... | collective-permute-start | bytes 196616 | tf_op jit(solution)/shard_map/ppermute | solution.py:548
  151.7 4.5 %collective-permute-start.14 = (bf16[1,8,16,256]{3,2,1,0:T(8,128)(2,1)S(1)}, bf16[1,8,16,256]{3,2,1,0:T(8,128)(2,1)S(1)}, u32[]{:S(2)}, u32[]{:S(2)}) collective-permute-start(bf16[1,8,16,256]{3,2,1,0:T(8,128)(2,1)S(1)} %get-tuple-element.82), channel_id=1, source_target_pairs={{0,24},{8,0},{16,8},{24,16},{1,25},{9,1},{17,9},{25,17},{2,26},{10... | collective-permute-start | bytes 196616 | tf_op jit(solution)/shard_map/ppermute | solution.py:548
  156.3 4.5 %collective-permute-start.15 = (bf16[4,32,256]{2,1,0:T(8,128)(2,1)S(1)}, bf16[4,32,256]{2,1,0:T(8,128)(2,1)S(1)}, u32[]{:S(2)}, u32[]{:S(2)}) collective-permute-start(bf16[4,32,256]{2,1,0:T(8,128)(2,1)S(1)} %get-tuple-element.84), channel_id=1, source_target_pairs={{0,32},{32,0},{64,96},{96,64},{128,160},{160,128},{192,224},{224,1... | collective-permute-start | bytes 196616 | tf_op jit(solution)/shard_map/ppermute | solution.py:600
  160.8 8.1 %collective-permute-start.16 = (bf16[1,32,256]{2,1,0:T(8,128)(2,1)S(1)}, bf16[1,32,256]{2,1,0:T(8,128)(2,1)S(1)}, u32[]{:S(2)}, u32[]{:S(2)}) collective-permute-start(bf16[1,32,256]{2,1,0:T(8,128)(2,1)S(1)} %get-tuple-element.86), channel_id=1, source_target_pairs={{0,64},{32,96},{64,128},{96,160},{128,192},{160,224},{192,0},{224,... | collective-permute-start | bytes 49160 | tf_op jit(solution)/shard_map/ppermute | solution.py:548
  160.9 8.0 %collective-permute-start.17 = (bf16[1,32,256]{2,1,0:T(8,128)(2,1)S(1)}, bf16[1,32,256]{2,1,0:T(8,128)(2,1)S(1)}, u32[]{:S(2)}, u32[]{:S(2)}) collective-permute-start(bf16[1,32,256]{2,1,0:T(8,128)(2,1)S(1)} %get-tuple-element.87), channel_id=1, source_target_pairs={{0,128},{32,160},{64,192},{96,224},{128,0},{160,32},{192,64},{224,... | collective-permute-start | bytes 49160 | tf_op jit(solution)/shard_map/ppermute | solution.py:548
  166.1 4.6 %collective-permute-start.18 = (bf16[1,32,256]{2,1,0:T(8,128)(2,1)S(1)}, bf16[1,32,256]{2,1,0:T(8,128)(2,1)S(1)}, u32[]{:S(2)}, u32[]{:S(2)}) collective-permute-start(bf16[1,32,256]{2,1,0:T(8,128)(2,1)S(1)} %get-tuple-element.88), channel_id=1, source_target_pairs={{0,192},{32,224},{64,0},{96,32},{128,64},{160,96},{192,128},{224,1... | collective-permute-start | bytes 49160 | tf_op jit(solution)/shard_map/ppermute | solution.py:548
  170.7 4.3 %collective-permute-start.21 = (bf16[32,256]{1,0:T(8,128)(2,1)S(1)}, bf16[32,256]{1,0:T(8,128)(2,1)S(1)}, u32[]{:S(2)}, u32[]{:S(2)}) collective-permute-start(bf16[32,256]{1,0:T(8,128)(2,1)S(1)} %bitcast.36), channel_id=1, source_target_pairs={{0,3},{1,0},{2,1},{3,2},{4,7},{5,4},{6,5},{7,6},{8,11},{9,8},{10,9... | collective-permute-start | bytes 49160 | tf_op jit(solution)/shard_map/ppermute | solution.py:548
  171.4 5.4 %collective-permute-start.20 = (bf16[32,256]{1,0:T(8,128)(2,1)S(1)}, bf16[32,256]{1,0:T(8,128)(2,1)S(1)}, u32[]{:S(2)}, u32[]{:S(2)}) collective-permute-start(bf16[32,256]{1,0:T(8,128)(2,1)S(1)} %bitcast.37), channel_id=1, source_target_pairs={{0,2},{1,3},{2,0},{3,1},{4,6},{5,7},{6,4},{7,5},{8,10},{9,11},{10,... | collective-permute-start | bytes 49160 | tf_op jit(solution)/shard_map/ppermute | solution.py:548
  175.1 4.9 %collective-permute-start.19 = (bf16[32,256]{1,0:T(8,128)(2,1)S(1)}, bf16[32,256]{1,0:T(8,128)(2,1)S(1)}, u32[]{:S(2)}, u32[]{:S(2)}) collective-permute-start(bf16[32,256]{1,0:T(8,128)(2,1)S(1)} %bitcast.38), channel_id=1, source_target_pairs={{0,1},{1,2},{2,3},{3,0},{4,5},{5,6},{6,7},{7,4},{8,9},{9,10},{10,1... | collective-permute-start | bytes 49160 | tf_op jit(solution)/shard_map/ppermute | solution.py:548
